TPU v7x, 256 devices: a whole 4x4x8 slice. The times are simulated.
256 devices in a mesh: span: 16 (over x, y_hi, core), tok: 16 (over z, y_lo).
Axes of the slice: x: 4, y: 4 (y_hi: 2, y_lo: 2; y = y_hi * 2 + y_lo), z: 8, core: 2. Of those that a mesh axis runs over, the one named last changes fastest.
Arguments:
- tokens: bfloat16 [131072, 256], P(('span', 'tok')), may hold values from -6 to 6
- w_in: bfloat16 [256, 768], replicated, may hold values from -0.375 to 0.375
- short_filter: float32 [3, 768], replicated, may hold values from -3 to 3
- long_filter: bfloat16 [256, 8192], P('tok'), may hold values from -0.0625 to 0.0625
- skip_gain: float32 [256], P('tok'), may hold values from 0.5 to 1.5
- w_out: bfloat16 [256, 256], replicated, may hold values from -0.375 to 0.375
Outputs:
- output: bfloat16 [131072, 256], P(('span', 'tok'))
All inputs are finite; a program needn't handle non-finite values.
Results may differ from a plain program's by a relative error of at most 0.0081.
Values may be sent and summed in bfloat16 or wider, within the bound.
No kernel may reach another device: no remote copies, remote signals or barrier semaphores. Data moves between devices by JAX's collectives and lax.ppermute only.
A program may use at most 64 MiB of HBM per device.

v0:
```python
import jax
import jax.numpy as jnp
from jax import lax
from jax.sharding import PartitionSpec as P

D = 256
BLOCK = 128


def passed_along(array, axis, by):
    peers = lax.axis_size(axis)
    pairs = [(i, i + by) for i in range(peers) if 0 <= i + by < peers]
    return lax.ppermute(array, axis, pairs)


def channel_conv(history_row, filter_row, taps_count, span_len):
    lag_blocks = taps_count // BLOCK + 1
    out_blocks = span_len // BLOCK
    in_blocks = lag_blocks - 1 + out_blocks
    padded_filter = jnp.concatenate(
        [jnp.zeros((BLOCK,), jnp.bfloat16), filter_row, jnp.zeros((BLOCK + 1,), jnp.bfloat16)]
    )
    period = padded_filter.shape[0]
    tiled = jnp.tile(padded_filter, BLOCK)[: BLOCK * (period - 1)].reshape(BLOCK, period - 1)
    toeplitz = tiled[:, BLOCK:].reshape(BLOCK, lag_blocks, BLOCK)
    block_rows = history_row.reshape(in_blocks, BLOCK)
    windows = jnp.tile(block_rows, (lag_blocks + 1, 1))[: lag_blocks * (in_blocks + 1)]
    windows = windows.reshape(lag_blocks, in_blocks + 1, BLOCK)[::-1, :out_blocks]
    conv_out = jnp.einsum("bja,jnb->na", toeplitz, windows, preferred_element_type=jnp.float32)
    return conv_out.reshape(span_len)


def per_device(tokens, w_in, short_filter, long_filter, skip_gain, w_out):
    tok_rows = tokens.shape[0]
    projected = lax.dot_general(
        w_in, tokens, (((0,), (1,)), ((), ())), preferred_element_type=jnp.float32
    ).astype(jnp.bfloat16)
    rim_cols = passed_along(projected[:, tok_rows - 2 :], ("span", "tok"), 1)
    padded = jnp.concatenate([rim_cols, projected], axis=1)
    padded = lax.optimization_barrier(padded).astype(jnp.float32)
    mixed = (
        short_filter[0][:, None] * padded[:, 2:]
        + short_filter[1][:, None] * padded[:, 1:-1]
        + short_filter[2][:, None] * padded[:, :-2]
    )
    query_rows = mixed[:D]
    key_rows = mixed[D : 2 * D]
    value_rows = mixed[2 * D :]
    product = (key_rows * value_rows).astype(jnp.bfloat16)
    span_len = tok_rows * lax.axis_size("tok")
    taps_count = long_filter.shape[1]
    local_chan = lax.all_to_all(product, "tok", split_axis=0, concat_axis=1, tiled=True)
    tail_list = [passed_along(local_chan, "span", 1)]
    history = jnp.concatenate(tail_list[::-1] + [local_chan], axis=1)

    def channel_step(carry, inputs):
        history_row, filter_row, gain_value = inputs
        conv_row = channel_conv(history_row, filter_row, taps_count, span_len)
        conv_row = conv_row + gain_value * history_row[taps_count:].astype(jnp.float32)
        return (carry, conv_row.astype(jnp.bfloat16))

    _, result = lax.scan(
        channel_step, jnp.zeros((), jnp.float32), (history, long_filter, skip_gain)
    )
    returned = lax.all_to_all(result, "tok", split_axis=1, concat_axis=0, tiled=True)
    returned = lax.optimization_barrier(returned).astype(jnp.float32)
    gated_rows = (query_rows * returned).astype(jnp.bfloat16)
    return lax.dot_general(
        gated_rows, w_out, (((0,), (0,)), ((), ())), preferred_element_type=jnp.float32
    ).astype(jnp.bfloat16)


def solution(mesh):
    return jax.shard_map(
        per_device,
        mesh=mesh,
        in_specs=(P(("span", "tok"), None), P(), P(), P("tok", None), P("tok"), P()),
        out_specs=P(("span", "tok"), None),
        check_vma=False,
    )
```

profile of v0, /device:TPU:6, one launch (start us, length us, event | category | flops | bytes accessed | tf_op | source)
XLA Modules:
  0.0 445.8 jit_solution(15623825728826733610)
XLA Ops:
  2.3 3.5 collective-permute-start
  6.7 6.8 %collective-permute-done = bf16[768,2]{0,1:T(2,128)(2,1)S(1)} collective-permute-done((bf16[768,2]{0,1:T(2,128)(2,1)S(1)}, bf16[768,2]{0,1:T(2,128)(2,1)S(1)}, u32[]{:S(2)}, u32[]{:S(2)}) %collective-permute-start) | collective-permute-done | bytes 3104 | tf_op jit(solution)/shard_map/ppermute | solution.py:13
  15.7 15.8 %all_to_all.38 = bf16[16,16,512]{2,1,0:T(8,128)(2,1)S(1)} all-to-all(bf16[16,16,512]{2,1,0:T(8,128)(2,1)S(1)} %bitcast.41), channel_id=1, replica_groups=mesh['span'=16,'tok'=16] {'tok'}, dimensions={0} | all-to-all | bytes 524288 | tf_op jit(solution)/shard_map/all_to_all | solution.py:52
  33.4 8.2 %collective-permute-done.1 = bf16[16,8192]{1,0:T(8,128)(2,1)S(1)} collective-permute-done((bf16[16,8192]{1,0:T(8,128)(2,1)S(1)}, bf16[16,8192]{1,0:T(8,128)(2,1)S(1)}, u32[]{:S(2)}, u32[]{:S(2)}) %collective-permute-start.1) | collective-permute-done | bytes 262176 | tf_op jit(solution)/shard_map/ppermute | solution.py:13
  41.6 388.2 %while.10 = (s32[]{:T(128)}, bf16[16,8192]{1,0:T(8,128)(2,1)S(1)}, bf16[16,16384]{1,0:T(8,128)(2,1)S(1)}, bf16[16,8192]{1,0:T(8,128)(2,1)}, f32[16]{0:T(128)S(1)}, /*index=5*/s32[]{:T(128)}, bf16[]{:T(256)}, s32[]{:T(128)}, s32[]{}) while((s32[]{:T(128)}, bf16[16,8192]{1,0:T(8,128)(2,1)S(1)}, bf16[16,16384]{1,0:T(8,128)(2,1)S(1)}, ...), condition=%wide.region_1.2_spmd, body=%wide.region_0.1_spmd.sunk | while | flops 136398336 | bytes 47534048 | solution.py:62
  48.0 4.1 tile.24
  53.8 3.5 reshape.39
  72.3 4.1 tile.24
  78.1 3.5 reshape.39
  96.6 4.1 tile.24
  102.3 3.5 reshape.39
  120.8 4.1 tile.24
  126.6 3.5 reshape.39
  145.1 4.1 tile.24
  150.9 3.5 reshape.39
  169.4 4.1 tile.24
  175.1 3.5 reshape.39
  193.6 4.1 tile.24
  199.4 3.5 reshape.39
  217.9 4.1 tile.24
  223.7 3.5 reshape.39
  242.2 4.1 tile.24
  247.9 3.5 reshape.39
  266.4 4.1 tile.24
  272.2 3.5 reshape.39
  290.7 4.1 tile.24
  315.0 4.1 tile.24
  339.2 4.1 tile.24
  363.5 4.1 tile.24
  387.8 4.1 tile.24
  412.0 4.1 tile.24
  429.9 13.7 %all_to_all.39 = bf16[16,16,512]{2,0,1:T(8,128)(2,1)S(1)} all-to-all(bf16[16,16,512]{2,0,1:T(8,128)(2,1)S(1)} %bitcast.43), channel_id=1, replica_groups=mesh['span'=16,'tok'=16] {'tok'}, dimensions={1} | all-to-all | bytes 524288 | tf_op jit(solution)/shard_map/all_to_all | solution.py:65
  (365 shorter events, 295.6 us)
Async XLA Ops:
  2.3 11.2 %collective-permute-start = (bf16[768,2]{0,1:T(2,128)(2,1)S(1)}, bf16[768,2]{0,1:T(2,128)(2,1)S(1)}, u32[]{:S(2)}, u32[]{:S(2)}) collective-permute-start(bf16[768,2]{0,1:T(2,128)(2,1)S(1)} %slice.60), channel_id=1, source_target_pairs={{0,1},{1,2},{2,3},{3,4},{4,5},{5,6},{6,7},{7,8},{8,9},{9,10},{10,1... | collective-permute-start | bytes 9224 | tf_op jit(solution)/shard_map/ppermute | solution.py:13
  15.5 26.1 %copy-start.3 = (f32[16]{0:T(128)S(1)}, f32[16]{0:T(128)}, u32[]{:S(2)}) copy-start(f32[16]{0:T(128)} %param.12) | copy-start | bytes 196
  31.5 10.1 %collective-permute-start.1 = (bf16[16,8192]{1,0:T(8,128)(2,1)S(1)}, bf16[16,8192]{1,0:T(8,128)(2,1)S(1)}, u32[]{:S(2)}, u32[]{:S(2)}) collective-permute-start(bf16[16,8192]{1,0:T(8,128)(2,1)S(1)} %bitcast.45), channel_id=1, source_target_pairs={{0,16},{16,32},{32,48},{48,64},{64,80},{80,96},{96,112},{112,128},... | collective-permute-start | bytes 786440 | tf_op jit(solution)/shard_map/ppermute | solution.py:13
  52.2 1.6 slice-start
  57.2 1.6 slice-start.1
  76.4 1.6 slice-start
  81.5 1.6 slice-start.1
  100.7 1.6 slice-start
  105.8 1.6 slice-start.1
  125.0 1.6 slice-start
  130.0 1.6 slice-start.1
  149.2 1.6 slice-start
  154.3 1.6 slice-start.1
  173.5 1.6 slice-start
  178.6 1.6 slice-start.1
  197.8 1.6 slice-start
  202.8 1.6 slice-start.1
  222.0 1.6 slice-start
  227.1 1.6 slice-start.1
  246.3 1.6 slice-start
  251.4 1.6 slice-start.1
  270.6 1.6 slice-start
  275.6 1.6 slice-start.1
  294.8 1.6 slice-start
  299.9 1.6 slice-start.1
  319.1 1.6 slice-start
  324.2 1.6 slice-start.1
  343.4 1.6 slice-start
  367.6 1.6 slice-start
  391.9 1.6 slice-start
  416.2 1.6 slice-start
  429.9 13.9 %copy-start.2 = (bf16[256,256]{1,0:T(8,128)(2,1)S(1)}, bf16[256,256]{1,0:T(8,128)(2,1)}, u32[]{:S(2)}) copy-start(bf16[256,256]{1,0:T(8,128)(2,1)} %param.13) | copy-start | bytes 393220
  (22 other events, 28.2 us)
where the time goes:
time: 448 us; the launch traced here: 446 us
  local copies, waits for them, and re-layouts  334 us (75%)
  matrix products  47.7 us (11%)
  blocking collectives  29.5 us (7%)
  waiting for transfers between devices  15 us (3%)
  other arithmetic  12.6 us (3%)
  starting transfers between devices  5.4 us (1%)
    another operation x32, local copies, waits for them, and re-layouts, channel_conv(): jnp.tile(padded_filter, BLOCK)[:BLOCK * (period - 1)]  68.6 us
    slice x48, local copies, waits for them, and re-layouts, channel_conv(): toeplitz = tiled[:, BLOCK:].reshape(BLOCK, lag_blocks, BLOCK)  64.4 us
    reshape x16, local copies, waits for them, and re-layouts, channel_conv(): jnp.tile(padded_filter, BLOCK)[:BLOCK * (period - 1)]  55.2 us
    dot_general x16, matrix products, channel_conv(): jnp.einsum('bja,jnb->na', toeplitz, windows, preferred_element_type=jnp.f...  44.4 us
    reshape x16, local copies, waits for them, and re-layouts, channel_conv(): windows.reshape(lag_blocks, in_blocks + 1, BLOCK)[::-1, :out_blocks]  31.7 us
    dynamic_slice x48, local copies, waits for them, and re-layouts, per_device(): lax.scan(channel_step, jnp.zeros((), jnp.float32), (history, long_filter,...  29.6 us
    slice x32, local copies, waits for them, and re-layouts, channel_conv(): jnp.tile(padded_filter, BLOCK)[:BLOCK * (period - 1)]  25.7 us
    slice x32, local copies, waits for them, and re-layouts, channel_conv(): windows.reshape(lag_blocks, in_blocks + 1, BLOCK)[::-1, :out_blocks]  19.7 us
  transfers between devices with their start and end apart: 2, of which 2 were waited for; matrix products, arithmetic and copies ran while one was open for 0% of the time, Pallas kernels for 0%

commit v1 on v0

v1 whole, which is shorter than its diff:
```python
import jax
import jax.numpy as jnp
import numpy as np
from jax import lax
from jax.experimental import pallas as pl
from jax.experimental.pallas import tpu as pltpu
from jax.sharding import PartitionSpec as P

D = 256
LANES = 128
HALF = 64
RIM = 16
POINTS = LANES * LANES


def dft_tables():
    ka = np.arange(HALF) + 0.5
    idx = np.arange(LANES)
    wave = lambda phase: np.exp(-2j * np.pi * phase)
    rows = wave(np.outer(ka, idx) / LANES)
    twist = wave(np.outer(ka, idx) / POINTS)
    cols = wave(np.outer(idx, idx) / LANES)
    into = np.concatenate([rows.real, rows.imag], 0)
    back = into.T[HALF:] * (2.0 / POINTS)
    cols_in = np.block([[cols.real, cols.imag], [-cols.imag, cols.real]])
    cols_out = np.block([[cols.real.T, -cols.imag.T], [cols.imag.T, cols.real.T]])
    bf = lambda a: jnp.asarray(a.astype(np.float32)).astype(jnp.bfloat16)
    twist = np.stack([twist.real, twist.imag]).astype(np.float32)
    return bf(into), bf(cols_in), bf(cols_out), bf(back), jnp.asarray(twist)


def dot(a, b):
    return jnp.dot(a, b, preferred_element_type=jnp.float32)


def project_kernel(tokens_ref, rim_ref, w_ref, taps_ref, product_ref, query_ref):
    rows = tokens_ref.shape[0]
    taps = taps_ref[...]

    def mixed(part):
        cols = slice(part * D, (part + 1) * D)
        weights = w_ref[:, cols]
        body = dot(tokens_ref[...], weights)
        head = dot(rim_ref[...], weights)
        both = jnp.concatenate([head, body], axis=0)
        both = both.astype(jnp.bfloat16).astype(jnp.float32)
        one = pltpu.roll(both, 1, axis=0)
        two = pltpu.roll(both, 2, axis=0)
        out = taps[0:1, cols] * both + taps[1:2, cols] * one + taps[2:3, cols] * two
        return out[RIM:]

    query_ref[...] = mixed(0)
    product = mixed(1) * mixed(2)
    product_ref[...] = jnp.transpose(product, (1, 0)).astype(jnp.bfloat16)


def project(tokens, rim, w_in, short_filter):
    rows = tokens.shape[0]
    return pl.pallas_call(
        project_kernel,
        out_shape=(
            jax.ShapeDtypeStruct((D, rows), jnp.bfloat16),
            jax.ShapeDtypeStruct((rows, D), jnp.float32),
        ),
        compiler_params=pltpu.CompilerParams(vmem_limit_bytes=24 << 20),
        cost_estimate=pl.CostEstimate(
            flops=2 * rows * D * 3 * D, bytes_accessed=2 << 20, transcendentals=0
        ),
        name="project",
    )(tokens, rim, w_in, short_filter)


def put_rows(load, scratch, chans, tiles, at):
    for tile in range(tiles):
        scratch[pl.ds((at + tile) * chans, chans), :] = load(tile).astype(jnp.float32)


def by_channel(scratch, chans, at, tiles):
    return jnp.concatenate(
        [scratch[pl.ds(at * chans + c, tiles, stride=chans), :] for c in range(chans)], axis=1
    )


def forward(into, cols_in, twist_re, twist_im, data, chans):
    first = dot(into, data)
    spun = []
    for c in range(chans):
        re = first[:HALF, c * LANES : (c + 1) * LANES]
        im = first[HALF:, c * LANES : (c + 1) * LANES]
        spun.append(
            jnp.concatenate(
                [re * twist_re - im * twist_im, re * twist_im + im * twist_re], axis=1
            ).astype(jnp.bfloat16)
        )
    return dot(jnp.concatenate(spun, axis=0), cols_in)


def spectrum_kernel(filter_ref, into_ref, cols_in_ref, twist_ref, out_ref, rows_ref):
    chans, taps = filter_ref.shape
    tiles = taps // LANES
    put_rows(lambda i: filter_ref[:, i * LANES : (i + 1) * LANES], rows_ref, chans, tiles, 0)
    data = by_channel(rows_ref, chans, 0, tiles).astype(jnp.bfloat16)
    out_ref[...] = forward(
        into_ref[:, :tiles], cols_in_ref[...], twist_ref[0], twist_ref[1], data, chans
    )


def spectrum(long_filter, into, cols_in, twist):
    chans, taps = long_filter.shape
    return pl.pallas_call(
        spectrum_kernel,
        out_shape=jax.ShapeDtypeStruct((chans * HALF, 2 * LANES), jnp.float32),
        scratch_shapes=[pltpu.VMEM((taps // LANES * chans, LANES), jnp.float32)],
        compiler_params=pltpu.CompilerParams(vmem_limit_bytes=24 << 20),
        cost_estimate=pl.CostEstimate(
            flops=400_000_000, bytes_accessed=3 << 20, transcendentals=0
        ),
        name="spectrum",
    )(long_filter, into, cols_in, twist)


def convolve_kernel(
    past_ref, own_ref, spec_ref, gain_ref, into_ref, cols_in_ref, cols_out_ref, back_ref,
    twist_ref, out_ref, rows_ref,
):
    peers, chans, width = own_ref.shape
    per = width // LANES
    tiles = peers * per
    twist_re = twist_ref[0]
    twist_im = twist_ref[1]

    def tile_of(ref):
        return lambda i: ref[i // per, :, (i % per) * LANES : (i % per + 1) * LANES]

    put_rows(tile_of(past_ref), rows_ref, chans, tiles, 0)
    put_rows(tile_of(own_ref), rows_ref, chans, tiles, tiles)
    data = by_channel(rows_ref, chans, 0, 2 * tiles)
    freq = forward(into_ref[...], cols_in_ref[...], twist_re, twist_im, data.astype(jnp.bfloat16), chans)
    spec = spec_ref[...]
    fre, fim = freq[:, :LANES], freq[:, LANES:]
    sre, sim = spec[:, :LANES], spec[:, LANES:]
    prod = jnp.concatenate([fre * sre - fim * sim, fre * sim + fim * sre], axis=1)
    last = dot(prod.astype(jnp.bfloat16), cols_out_ref[...])
    spun = []
    for c in range(chans):
        re = last[c * HALF : (c + 1) * HALF, :LANES]
        im = last[c * HALF : (c + 1) * HALF, LANES:]
        spun.append(
            jnp.concatenate(
                [re * twist_re + im * twist_im, im * twist_re - re * twist_im], axis=0
            ).astype(jnp.bfloat16)
        )
    result = dot(back_ref[...], jnp.concatenate(spun, axis=1))
    for c in range(chans):
        lanes = slice(c * LANES, (c + 1) * LANES)
        rows_ref[pl.ds(c, tiles, stride=chans), :] = (
            result[:, lanes] + gain_ref[c] * data[tiles:, lanes]
        )
    for tile in range(tiles):
        out_ref[tile // per, :, (tile % per) * LANES : (tile % per + 1) * LANES] = rows_ref[
            pl.ds(tile * chans, chans), :
        ].astype(jnp.bfloat16)


def convolve(past, own, spec, gain, into, cols_in, cols_out, back, twist):
    peers, chans, width = own.shape
    vmem = pl.BlockSpec(memory_space=pltpu.VMEM)
    return pl.pallas_call(
        convolve_kernel,
        out_shape=jax.ShapeDtypeStruct(own.shape, jnp.bfloat16),
        in_specs=[vmem, vmem, vmem, pl.BlockSpec(memory_space=pltpu.SMEM)] + [vmem] * 5,
        out_specs=vmem,
        scratch_shapes=[pltpu.VMEM((2 * peers * chans * width // LANES, LANES), jnp.float32)],
        compiler_params=pltpu.CompilerParams(vmem_limit_bytes=32 << 20),
        cost_estimate=pl.CostEstimate(
            flops=800_000_000, bytes_accessed=4 << 20, transcendentals=0
        ),
        name="convolve",
    )(past, own, spec, gain, into, cols_in, cols_out, back, twist)


def output_kernel(conv_ref, query_ref, w_ref, out_ref):
    conv = jnp.transpose(conv_ref[...].astype(jnp.float32), (1, 0))
    gated = (query_ref[...] * conv).astype(jnp.bfloat16)
    out_ref[...] = dot(gated, w_ref[...]).astype(jnp.bfloat16)


def project_out(conv, query, w_out):
    rows = query.shape[0]
    return pl.pallas_call(
        output_kernel,
        out_shape=jax.ShapeDtypeStruct((rows, D), jnp.bfloat16),
        compiler_params=pltpu.CompilerParams(vmem_limit_bytes=16 << 20),
        cost_estimate=pl.CostEstimate(
            flops=2 * rows * D * D, bytes_accessed=2 << 20, transcendentals=0
        ),
        name="project_out",
    )(conv, query, w_out)


def passed_along(array, axis):
    peers = lax.axis_size(axis)
    return lax.ppermute(array, axis, [(i, i + 1) for i in range(peers - 1)])


def per_device(tokens, w_in, short_filter, long_filter, skip_gain, w_out):
    rows = tokens.shape[0]
    peers = lax.axis_size("tok")
    into, cols_in, cols_out, back, twist = dft_tables()
    rim = passed_along(tokens[rows - RIM :], ("span", "tok"))
    product, query = project(tokens, rim, w_in, short_filter)
    own = lax.all_to_all(
        product.reshape(peers, D // peers, rows), "tok", split_axis=0, concat_axis=0, tiled=True
    )
    past = passed_along(own, "span")
    spec = spectrum(long_filter, into, cols_in, twist)
    conv = convolve(past, own, spec, skip_gain, into, cols_in, cols_out, back, twist)
    conv = lax.all_to_all(conv, "tok", split_axis=0, concat_axis=0, tiled=True)
    return project_out(conv.reshape(D, rows), query, w_out)


def solution(mesh):
    return jax.shard_map(
        per_device,
        mesh=mesh,
        in_specs=(P(("span", "tok"), None), P(), P(), P("tok", None), P("tok"), P()),
        out_specs=P(("span", "tok"), None),
        check_vma=False,
    )
```

time: 448 us -> 57.8 us (0.13)
  local copies, waits for them, and re-layouts: 334 us -> 2.7 us
  matrix products: 47.7 us -> 0 us
  other arithmetic: 12.6 us -> 0 us
    slice x130 -> x1, local copies, waits for them, and re-layouts: 114 us -> 0.71 us  [per_device(): rim = passed_along(tokens[rows - RIM:], ('span', 'tok'))]
    reshape x32 -> x0, local copies, waits for them, and re-layouts: 86.9 us -> none  [the longest x16 55.2 us: channel_conv(): jnp.tile(padded_filter, BLOCK)[:BLOCK * (period - 1)]]
    another operation x80 -> x0, local copies, waits for them, and re-layouts: 76.9 us -> none  [the longest x32 68.6 us: channel_conv(): jnp.tile(padded_filter, BLOCK)[:BLOCK * (period - 1)]]
    dot_general x18 -> x0, matrix products: 47.7 us -> none  [the longest x16 44.4 us: channel_conv(): jnp.einsum('bja,jnb->na', toeplitz, windows, preferred_element_type=jnp.f...]
    dynamic_slice x48 -> x0, local copies, waits for them, and re-layouts: 29.6 us -> none  [per_device(): lax.scan(channel_step, jnp.zeros((), jnp.float32), (history, long_filter,...]
    rev x16 -> x0, local copies, waits for them, and re-layouts: 16.8 us -> none  [channel_conv(): windows.reshape(lag_blocks, in_blocks + 1, BLOCK)[::-1, :out_blocks]]
    convert_element_type x18 -> x0, other arithmetic: 11.7 us -> none  [the longest x16 11.6 us: channel_step(): return (carry, conv_row.astype(jnp.bfloat16))]
    dynamic_update_slice x16 -> x0, local copies, waits for them, and re-layouts: 7.61 us -> none  [per_device(): lax.scan(channel_step, jnp.zeros((), jnp.float32), (history, long_filter,...]
  transfers between devices with their start and end apart: 2 -> 2, of which waited for: 2 -> 2; matrix products, arithmetic and copies ran while one was open for 0% -> 0% of each run, Pallas kernels for 0% -> 1%
where the time goes in v1:
time: 57.8 us; the launch traced here: 57.5 us
  blocking collectives  29.7 us (51%)
  waiting for transfers between devices  15.3 us (26%)
  starting transfers between devices  5.51 us (10%)
  Pallas kernels  4.13 us (7%)
  local copies, waits for them, and re-layouts  2.7 us (5%)
    all_to_all x1, blocking collectives, per_device(): lax.all_to_all(product.reshape(peers, D // peers, rows), 'tok', split_axi...  15.9 us
    ppermute x2, waiting for transfers between devices, passed_along(): return lax.ppermute(array, axis, [(i, i + 1) for i in range(peers - 1)])  15.3 us
    all_to_all x1, blocking collectives, per_device(): conv = lax.all_to_all(conv, 'tok', split_axis=0, concat_axis=0, tiled=True)  13.7 us
    ppermute x2, starting transfers between devices, passed_along(): return lax.ppermute(array, axis, [(i, i + 1) for i in range(peers - 1)])  5.51 us
    unnamed x22, local copies, waits for them, and re-layouts  1.99 us
    pallas_call x1, Pallas kernels, convolve(): pl.pallas_call(convolve_kernel, out_shape=jax.ShapeDtypeStruct(own.shape,...  1.67 us
  transfers between devices with their start and end apart: 2, of which 2 were waited for; matrix products, arithmetic and copies ran while one was open for 0% of the time, Pallas kernels for 1%

profile of v1, /device:TPU:6, one launch (start us, length us, event | category | flops | bytes accessed | tf_op | source)
XLA Modules:
  0.0 57.5 jit_solution(13079626622064715576)
XLA Ops:
  0.0 0.0 copy-start.7
  0.0 0.7 %slice.3 = bf16[16,256]{1,0:T(8,128)(2,1)S(1)} slice(bf16[512,256]{1,0:T(8,128)(2,1)} %tokens_ref.1), slice={[496:512], [0:256]} | slice | bytes 16384 | tf_op jit(solution)/shard_map/slice | solution.py:210
  0.7 3.5 %collective-permute-start = (bf16[16,256]{1,0:T(8,128)(2,1)S(1)}, bf16[16,256]{1,0:T(8,128)(2,1)S(1)}, u32[]{:S(2)}, u32[]{:S(2)}) collective-permute-start(bf16[16,256]{1,0:T(8,128)(2,1)S(1)} %slice.3), channel_id=1, source_target_pairs={{0,1},{1,2},{2,3},{3,4},{4,5},{5,6},{6,7},{7,8},{8,9},{9,10},{10,1... | collective-permute-start | bytes 24584 | tf_op jit(solution)/shard_map/ppermute | solution.py:203
  4.2 7.8 %collective-permute-done.rim_ref = bf16[16,256]{1,0:T(8,128)(2,1)S(1)} collective-permute-done((bf16[16,256]{1,0:T(8,128)(2,1)S(1)}, bf16[16,256]{1,0:T(8,128)(2,1)S(1)}, u32[]{:S(2)}, u32[]{:S(2)}) %collective-permute-start) | collective-permute-done | bytes 8224 | tf_op jit(solution)/shard_map/ppermute | solution.py:203
  12.0 0.0 copy-done.7
  12.0 0.0 copy-start.5
  12.0 0.9 %copy-done.5 = bf16[512,256]{1,0:T(8,128)(2,1)S(1)} copy-done((bf16[512,256]{1,0:T(8,128)(2,1)S(1)}, bf16[512,256]{1,0:T(8,128)(2,1)}, u32[]{:S(2)}) %copy-start.5) | copy-done | bytes 262168
  12.9 0.0 copy-start.6
  12.9 1.0 %copy-done.6 = bf16[256,768]{1,0:T(8,128)(2,1)S(1)} copy-done((bf16[256,768]{1,0:T(8,128)(2,1)S(1)}, bf16[256,768]{1,0:T(8,128)(2,1)}, u32[]{:S(2)}) %copy-start.6) | copy-done | bytes 393240
  13.9 0.9 %project.1 = (bf16[256,512]{1,0:T(8,128)(2,1)S(1)}, f32[512,256]{1,0:T(8,128)S(1)}) custom-call(bf16[512,256]{1,0:T(8,128)(2,1)S(1)} %copy-done.5, bf16[16,256]{1,0:T(8,128)(2,1)S(1)} %collective-permute-done.rim_ref, bf16[256,768]{1,0:T(8,128)(2,1)S(1)} %copy-done.6, f32[3,768]{1,0:T(4,128)S(1)} %copy-done.7), custom_call_target="tpu_custom_call" | custom-call | flops 201326592 | bytes 2097152 | tf_op jit(solution)/shard_map/project/pallas_call | solution.py:59
  14.8 0.0 copy-start
  14.9 0.0 copy-start.2
  14.9 0.0 copy-start.3
  14.9 0.0 copy-start.4
  14.9 15.9 %all_to_all.10.own_ref = bf16[16,16,512]{2,1,0:T(8,128)(2,1)S(1)} all-to-all(bf16[16,16,512]{2,1,0:T(8,128)(2,1)S(1)} %bitcast.3), channel_id=1, replica_groups=mesh['span'=16,'tok'=16] {'tok'}, dimensions={0} | all-to-all | bytes 524288 | tf_op jit(solution)/shard_map/all_to_all | solution.py:212
  30.8 0.0 copy-start.8
  30.8 0.0 copy-start.9
  30.8 2.0 %collective-permute-start.1 = (bf16[16,16,512]{2,1,0:T(8,128)(2,1)S(1)}, bf16[16,16,512]{2,1,0:T(8,128)(2,1)S(1)}, u32[]{:S(2)}, u32[]{:S(2)}) collective-permute-start(bf16[16,16,512]{2,1,0:T(8,128)(2,1)S(1)} %all_to_all.10.own_ref), channel_id=1, source_target_pairs={{0,16},{16,32},{32,48},{48,64},{64,80},{80,96},{96,112},{112,128},... | collective-permute-start | bytes 786440 | tf_op jit(solution)/shard_map/ppermute | solution.py:203
  32.9 0.0 copy-done
  32.9 0.0 copy-done.2
  32.9 0.0 copy-done.3
  32.9 0.0 copy-done.4
  32.9 0.5 spectrum.1.spec_ref
  33.4 7.6 %collective-permute-done.1.past_ref = bf16[16,16,512]{2,1,0:T(8,128)(2,1)S(1)} collective-permute-done((bf16[16,16,512]{2,1,0:T(8,128)(2,1)S(1)}, bf16[16,16,512]{2,1,0:T(8,128)(2,1)S(1)}, u32[]{:S(2)}, u32[]{:S(2)}) %collective-permute-start.1) | collective-permute-done | bytes 262176 | tf_op jit(solution)/shard_map/ppermute | solution.py:203
  41.0 0.0 copy-done.8
  41.0 0.0 copy-done.9
  41.0 0.0 copy-done.10
  41.0 1.7 %convolve.1 = bf16[16,16,512]{2,1,0:T(8,128)(2,1)S(1)} custom-call(bf16[16,16,512]{2,1,0:T(8,128)(2,1)S(1)} %collective-permute-done.1.past_ref, bf16[16,16,512]{2,1,0:T(8,128)(2,1)S(1)} %all_to_all.10.own_ref, f32[1024,256]{1,0:T(8,128)S(1)} %spectrum.1.spec_ref, f32[16]{0:T(128)S(1)} %copy-done.8, bf16[128,128]{1,0:T(8,128)(2,1)S(1)} %copy-done.4, ...), custom_call_target="tpu_custom_call" | custom-call | flops 800000000 | bytes 4194304 | tf_op jit(solution)/shard_map/convolve/pallas_call | solution.py:168
  42.7 0.0 copy-start.1
  42.7 13.7 %all_to_all.11 = bf16[16,16,512]{2,1,0:T(8,128)(2,1)S(1)} all-to-all(bf16[16,16,512]{2,1,0:T(8,128)(2,1)S(1)} %convolve.1), channel_id=1, replica_groups=mesh['span'=16,'tok'=16] {'tok'}, dimensions={0} | all-to-all | bytes 524288 | tf_op jit(solution)/shard_map/all_to_all | solution.py:218
  56.5 0.0 copy-done.1
  56.5 1.0 %project_out.1 = bf16[512,256]{1,0:T(8,128)(2,1)} custom-call(bf16[256,512]{1,0:T(8,128)(2,1)S(1)} %bitcast.2, f32[512,256]{1,0:T(8,128)S(1)} %get-tuple-element.8.query_ref, bf16[256,256]{1,0:T(8,128)(2,1)S(1)} %copy-done.1), custom_call_target="tpu_custom_call" | custom-call | flops 67108864 | bytes 2097152 | tf_op jit(solution)/shard_map/project_out/pallas_call | solution.py:190
  (1 shorter events, 0.0 us)
Async XLA Ops:
  0.0 12.0 %copy-start.7 = (f32[3,768]{1,0:T(4,128)S(1)}, f32[3,768]{1,0:T(4,128)}, u32[]{:S(2)}) copy-start(f32[3,768]{1,0:T(4,128)} %taps_ref.1) | copy-start | bytes 27652
  0.7 11.2 %collective-permute-start = (bf16[16,256]{1,0:T(8,128)(2,1)S(1)}, bf16[16,256]{1,0:T(8,128)(2,1)S(1)}, u32[]{:S(2)}, u32[]{:S(2)}) collective-permute-start(bf16[16,256]{1,0:T(8,128)(2,1)S(1)} %slice.3), channel_id=1, source_target_pairs={{0,1},{1,2},{2,3},{3,4},{4,5},{5,6},{6,7},{7,8},{8,9},{9,10},{10,1... | collective-permute-start | bytes 24584 | tf_op jit(solution)/shard_map/ppermute | solution.py:203
  12.0 1.0 %copy-start.5 = (bf16[512,256]{1,0:T(8,128)(2,1)S(1)}, bf16[512,256]{1,0:T(8,128)(2,1)}, u32[]{:S(2)}) copy-start(bf16[512,256]{1,0:T(8,128)(2,1)} %tokens_ref.1) | copy-start | bytes 786436
  12.9 1.0 %copy-start.6 = (bf16[256,768]{1,0:T(8,128)(2,1)S(1)}, bf16[256,768]{1,0:T(8,128)(2,1)}, u32[]{:S(2)}) copy-start(bf16[256,768]{1,0:T(8,128)(2,1)} %w_ref.2) | copy-start | bytes 1179652
  14.8 18.0 %copy-start = (bf16[16,8192]{1,0:T(8,128)(2,1)S(1)}, bf16[16,8192]{1,0:T(8,128)(2,1)}, u32[]{:S(2)}) copy-start(bf16[16,8192]{1,0:T(8,128)(2,1)} %filter_ref.1) | copy-start | bytes 786436
  14.9 18.0 %copy-start.2 = (bf16[256,256]{1,0:T(8,128)(2,1)S(1)}, bf16[256,256]{1,0:T(8,128)(2,1)}, u32[]{:S(2)}) copy-start(bf16[256,256]{1,0:T(8,128)(2,1)} %constant.16.cols_in_ref) | copy-start | bytes 393220
  14.9 18.0 %copy-start.3 = (f32[2,64,128]{2,1,0:T(8,128)S(1)}, f32[2,64,128]{2,1,0:T(8,128)}, u32[]{:S(2)}) copy-start(f32[2,64,128]{2,1,0:T(8,128)} %constant.14.clone.twist_ref) | copy-start | bytes 196612
  14.9 18.0 %copy-start.4 = (bf16[128,128]{1,0:T(8,128)(2,1)S(1)}, bf16[128,128]{1,0:T(8,128)(2,1)}, u32[]{:S(2)}) copy-start(bf16[128,128]{1,0:T(8,128)(2,1)} %constant.15.into_ref) | copy-start | bytes 98308
  30.8 10.2 %copy-start.8 = (f32[16]{0:T(128)S(1)}, f32[16]{0:T(128)}, u32[]{:S(2)}) copy-start(f32[16]{0:T(128)} %gain_ref.1) | copy-start | bytes 196
  30.8 10.2 %copy-start.9 = (bf16[256,256]{1,0:T(8,128)(2,1)S(1)}, bf16[256,256]{1,0:T(8,128)(2,1)}, u32[]{:S(2)}) copy-start(bf16[256,256]{1,0:T(8,128)(2,1)} %constant.17.cols_out_ref) | copy-start | bytes 393220
  30.8 10.2 %copy-start.10 = (bf16[64,128]{1,0:T(8,128)(2,1)S(1)}, bf16[64,128]{1,0:T(8,128)(2,1)}, u32[]{:S(2)}) copy-start(bf16[64,128]{1,0:T(8,128)(2,1)} %constant.18.back_ref) | copy-start | bytes 49156
  30.8 10.2 %collective-permute-start.1 = (bf16[16,16,512]{2,1,0:T(8,128)(2,1)S(1)}, bf16[16,16,512]{2,1,0:T(8,128)(2,1)S(1)}, u32[]{:S(2)}, u32[]{:S(2)}) collective-permute-start(bf16[16,16,512]{2,1,0:T(8,128)(2,1)S(1)} %all_to_all.10.own_ref), channel_id=1, source_target_pairs={{0,16},{16,32},{32,48},{48,64},{64,80},{80,96},{96,112},{112,128},... | collective-permute-start | bytes 786440 | tf_op jit(solution)/shard_map/ppermute | solution.py:203
  42.7 13.8 %copy-start.1 = (bf16[256,256]{1,0:T(8,128)(2,1)S(1)}, bf16[256,256]{1,0:T(8,128)(2,1)}, u32[]{:S(2)}) copy-start(bf16[256,256]{1,0:T(8,128)(2,1)} %w_ref.3) | copy-start | bytes 393220

commit v2 on v1

--- a/solution.py
+++ b/solution.py
@@ -33,41 +33,98 @@
     return jnp.dot(a, b, preferred_element_type=jnp.float32)
 
 
-def project_kernel(tokens_ref, rim_ref, w_ref, taps_ref, product_ref, query_ref):
-    rows = tokens_ref.shape[0]
-    taps = taps_ref[...]
+VMEM = pl.BlockSpec(memory_space=pltpu.VMEM)
+SMEM = pl.BlockSpec(memory_space=pltpu.SMEM)
+HBM = pl.BlockSpec(memory_space=pltpu.MemorySpace.HBM)
+HEAD = 8
+
+
+def short_filter_sum(taps, now, one, two):
+    return taps[0:1] * now + taps[1:2] * one + taps[2:3] * two
+
+
+def rounded(projected):
+    return projected.astype(jnp.bfloat16).astype(jnp.float32)
+
+
+def project_kernel(
+    tokens_hbm, w_hbm, taps_hbm, product_ref, query_ref, head_ref, w_ref, taps_ref, tokens_ref, sems
+):
+    copies = [
+        pltpu.make_async_copy(tokens_hbm, tokens_ref, sems.at[0]),
+        pltpu.make_async_copy(w_hbm, w_ref, sems.at[1]),
+        pltpu.make_async_copy(taps_hbm, taps_ref, sems.at[2]),
+    ]
+    for copy in copies:
+        copy.start()
+    for copy in copies:
+        copy.wait()
 
     def mixed(part):
         cols = slice(part * D, (part + 1) * D)
-        weights = w_ref[:, cols]
-        body = dot(tokens_ref[...], weights)
-        head = dot(rim_ref[...], weights)
-        both = jnp.concatenate([head, body], axis=0)
-        both = both.astype(jnp.bfloat16).astype(jnp.float32)
-        one = pltpu.roll(both, 1, axis=0)
-        two = pltpu.roll(both, 2, axis=0)
-        out = taps[0:1, cols] * both + taps[1:2, cols] * one + taps[2:3, cols] * two
-        return out[RIM:]
-
-    query_ref[...] = mixed(0)
+        now = rounded(dot(tokens_ref[...], w_ref[:, cols]))
+        head_ref[:, cols] = now[:HEAD]
+        return short_filter_sum(
+            taps_ref[:, cols], now, pltpu.roll(now, 1, axis=0), pltpu.roll(now, 2, axis=0)
+        )
+
     product = mixed(1) * mixed(2)
     product_ref[...] = jnp.transpose(product, (1, 0)).astype(jnp.bfloat16)
-
-
-def project(tokens, rim, w_in, short_filter):
+    query_ref[...] = mixed(0)
+
+
+def project(tokens, w_in, short_filter):
     rows = tokens.shape[0]
     return pl.pallas_call(
         project_kernel,
         out_shape=(
             jax.ShapeDtypeStruct((D, rows), jnp.bfloat16),
             jax.ShapeDtypeStruct((rows, D), jnp.float32),
-        ),
+            jax.ShapeDtypeStruct((HEAD, 3 * D), jnp.float32),
+            jax.ShapeDtypeStruct(w_in.shape, w_in.dtype),
+            jax.ShapeDtypeStruct(short_filter.shape, short_filter.dtype),
+        ),
+        in_specs=[HBM] * 3,
+        out_specs=(VMEM,) * 5,
+        scratch_shapes=[pltpu.VMEM(tokens.shape, tokens.dtype), pltpu.SemaphoreType.DMA((3,))],
         compiler_params=pltpu.CompilerParams(vmem_limit_bytes=24 << 20),
         cost_estimate=pl.CostEstimate(
             flops=2 * rows * D * 3 * D, bytes_accessed=2 << 20, transcendentals=0
         ),
         name="project",
-    )(tokens, rim, w_in, short_filter)
+    )(tokens, w_in, short_filter)
+
+
+def rim_kernel(place_ref, rim_ref, w_ref, taps_ref, head_ref, raw_ref, product_ref, query_ref):
+    there = place_ref[0] + place_ref[1] > 0
+    before = rounded(dot(rim_ref[...], w_ref[...]))[RIM - HEAD :]
+    before = jnp.where(there, before, 0.0)
+    both = jnp.concatenate([before, head_ref[...]], axis=0)
+    mixed = short_filter_sum(
+        taps_ref[...], both, pltpu.roll(both, 1, axis=0), pltpu.roll(both, 2, axis=0)
+    )[HEAD:]
+    query_ref[...] = mixed[:, :D]
+    fixed = mixed[:, D : 2 * D] * mixed[:, 2 * D :]
+    fixed = jnp.concatenate([fixed, jnp.zeros((LANES - HEAD, D), jnp.float32)], axis=0)
+    fixed = jnp.transpose(fixed, (1, 0)).astype(jnp.bfloat16)
+    lane = lax.broadcasted_iota(jnp.int32, fixed.shape, 1)
+    product_ref[:, LANES:] = raw_ref[:, LANES:]
+    product_ref[:, :LANES] = jnp.where(lane < HEAD, fixed, raw_ref[:, :LANES])
+
+
+def fix_rim(place, rim, w_in, short_filter, head, product):
+    return pl.pallas_call(
+        rim_kernel,
+        out_shape=(
+            jax.ShapeDtypeStruct(product.shape, product.dtype),
+            jax.ShapeDtypeStruct((HEAD, D), jnp.float32),
+        ),
+        in_specs=[SMEM] + [VMEM] * 5,
+        out_specs=(VMEM, VMEM),
+        compiler_params=pltpu.CompilerParams(vmem_limit_bytes=16 << 20),
+        cost_estimate=pl.CostEstimate(flops=20_000_000, bytes_accessed=1 << 20, transcendentals=0),
+        name="fix_rim",
+    )(place, rim, w_in, short_filter, head, product)
 
 
 def put_rows(load, scratch, chans, tiles, at):
@@ -120,7 +177,7 @@
 
 
 def convolve_kernel(
-    past_ref, own_ref, spec_ref, gain_ref, into_ref, cols_in_ref, cols_out_ref, back_ref,
+    place_ref, past_ref, own_ref, spec_ref, gain_ref, into_ref, cols_in_ref, cols_out_ref, back_ref,
     twist_ref, out_ref, rows_ref,
 ):
     peers, chans, width = own_ref.shape
@@ -133,6 +190,11 @@
         return lambda i: ref[i // per, :, (i % per) * LANES : (i % per + 1) * LANES]
 
     put_rows(tile_of(past_ref), rows_ref, chans, tiles, 0)
+
+    @pl.when(place_ref[0] == 0)
+    def _():
+        rows_ref[: tiles * chans] = jnp.zeros((tiles * chans, LANES), jnp.float32)
+
     put_rows(tile_of(own_ref), rows_ref, chans, tiles, tiles)
     data = by_channel(rows_ref, chans, 0, 2 * tiles)
     freq = forward(into_ref[...], cols_in_ref[...], twist_re, twist_im, data.astype(jnp.bfloat16), chans)
@@ -162,30 +224,30 @@
         ].astype(jnp.bfloat16)
 
 
-def convolve(past, own, spec, gain, into, cols_in, cols_out, back, twist):
+def convolve(place, past, own, spec, gain, into, cols_in, cols_out, back, twist):
     peers, chans, width = own.shape
-    vmem = pl.BlockSpec(memory_space=pltpu.VMEM)
     return pl.pallas_call(
         convolve_kernel,
         out_shape=jax.ShapeDtypeStruct(own.shape, jnp.bfloat16),
-        in_specs=[vmem, vmem, vmem, pl.BlockSpec(memory_space=pltpu.SMEM)] + [vmem] * 5,
-        out_specs=vmem,
+        in_specs=[SMEM] + [VMEM] * 3 + [SMEM] + [VMEM] * 5,
+        out_specs=VMEM,
         scratch_shapes=[pltpu.VMEM((2 * peers * chans * width // LANES, LANES), jnp.float32)],
         compiler_params=pltpu.CompilerParams(vmem_limit_bytes=32 << 20),
         cost_estimate=pl.CostEstimate(
             flops=800_000_000, bytes_accessed=4 << 20, transcendentals=0
         ),
         name="convolve",
-    )(past, own, spec, gain, into, cols_in, cols_out, back, twist)
-
-
-def output_kernel(conv_ref, query_ref, w_ref, out_ref):
+    )(place, past, own, spec, gain, into, cols_in, cols_out, back, twist)
+
+
+def output_kernel(conv_ref, query_ref, head_ref, w_ref, out_ref):
     conv = jnp.transpose(conv_ref[...].astype(jnp.float32), (1, 0))
-    gated = (query_ref[...] * conv).astype(jnp.bfloat16)
+    query = jnp.concatenate([head_ref[...], query_ref[HEAD:]], axis=0)
+    gated = (query * conv).astype(jnp.bfloat16)
     out_ref[...] = dot(gated, w_ref[...]).astype(jnp.bfloat16)
 
 
-def project_out(conv, query, w_out):
+def project_out(conv, query, head, w_out):
     rows = query.shape[0]
     return pl.pallas_call(
         output_kernel,
@@ -195,28 +257,30 @@
             flops=2 * rows * D * D, bytes_accessed=2 << 20, transcendentals=0
         ),
         name="project_out",
-    )(conv, query, w_out)
-
-
-def passed_along(array, axis):
-    peers = lax.axis_size(axis)
-    return lax.ppermute(array, axis, [(i, i + 1) for i in range(peers - 1)])
+    )(conv, query, head, w_out)
+
+
+def rotated(array, axes):
+    count = lax.axis_size(axes)
+    return lax.ppermute(array, axes, [(i, (i + 1) % count) for i in range(count)])
 
 
 def per_device(tokens, w_in, short_filter, long_filter, skip_gain, w_out):
     rows = tokens.shape[0]
     peers = lax.axis_size("tok")
     into, cols_in, cols_out, back, twist = dft_tables()
-    rim = passed_along(tokens[rows - RIM :], ("span", "tok"))
-    product, query = project(tokens, rim, w_in, short_filter)
+    place = jnp.stack([lax.axis_index("span"), lax.axis_index("tok")]).astype(jnp.int32)
+    rim = rotated(tokens[rows - RIM :], ("span", "tok"))
+    product, query, head, w_copy, taps = project(tokens, w_in, short_filter)
+    product, query_head = fix_rim(place, rim, w_copy, taps, head, product)
     own = lax.all_to_all(
         product.reshape(peers, D // peers, rows), "tok", split_axis=0, concat_axis=0, tiled=True
     )
-    past = passed_along(own, "span")
+    past = rotated(own, "span")
     spec = spectrum(long_filter, into, cols_in, twist)
-    conv = convolve(past, own, spec, skip_gain, into, cols_in, cols_out, back, twist)
+    conv = convolve(place, past, own, spec, skip_gain, into, cols_in, cols_out, back, twist)
     conv = lax.all_to_all(conv, "tok", split_axis=0, concat_axis=0, tiled=True)
-    return project_out(conv.reshape(D, rows), query, w_out)
+    return project_out(conv.reshape(D, rows), query, query_head, w_out)
 
 
 def solution(mesh):

time: 57.8 us -> 52 us (0.90)
  starting transfers between devices: 5.51 us -> 1.58 us
  waiting for transfers between devices: 15.3 us -> 12.2 us
  Pallas kernels: 4.13 us -> 5.2 us
    ppermute x2, starting transfers between devices: 5.51 us -> 1.58 us  [rotated(): lax.ppermute(array, axes, [(i, (i + 1) % count) for i in range(count)])]
    ppermute x2, waiting for transfers between devices: 15.3 us -> 12.2 us  [rotated(): lax.ppermute(array, axes, [(i, (i + 1) % count) for i in range(count)])]
    pallas_call x0 -> x1, Pallas kernels: none -> 0.83 us  [fix_rim(): pl.pallas_call(rim_kernel, out_shape=(jax.ShapeDtypeStruct(product.shape,...]
  transfers between devices with their start and end apart: 2 -> 2, of which waited for: 2 -> 2; matrix products, arithmetic and copies ran while one was open for 0% -> 0% of each run, Pallas kernels for 1% -> 3%
where the time goes in v2:
time: 52 us; the launch traced here: 51.7 us
  blocking collectives  29.9 us (58%)
  waiting for transfers between devices  12.2 us (23%)
  Pallas kernels  5.2 us (10%)
  local copies, waits for them, and re-layouts  2.69 us (5%)
  starting transfers between devices  1.58 us (3%)
    all_to_all x1, blocking collectives, per_device(): lax.all_to_all(product.reshape(peers, D // peers, rows), 'tok', split_axi...  16.2 us
    all_to_all x1, blocking collectives, per_device(): conv = lax.all_to_all(conv, 'tok', split_axis=0, concat_axis=0, tiled=True)  13.7 us
    ppermute x2, waiting for transfers between devices, rotated(): lax.ppermute(array, axes, [(i, (i + 1) % count) for i in range(count)])  12.2 us
    unnamed x22, local copies, waits for them, and re-layouts  1.99 us
    pallas_call x1, Pallas kernels, convolve(): pl.pallas_call(convolve_kernel, out_shape=jax.ShapeDtypeStruct(own.shape,...  1.68 us
    ppermute x2, starting transfers between devices, rotated(): lax.ppermute(array, axes, [(i, (i + 1) % count) for i in range(count)])  1.58 us
    pallas_call x1, Pallas kernels, project(): pl.pallas_call(project_kernel, out_shape=(jax.ShapeDtypeStruct((D, rows),...  1.16 us
  transfers between devices with their start and end apart: 2, of which 2 were waited for; matrix products, arithmetic and copies ran while one was open for 0% of the time, Pallas kernels for 3%

profile of v2, /device:TPU:6, one launch (start us, length us, event | category | flops | bytes accessed | tf_op | source)
XLA Modules:
  0.0 51.7 jit_solution(1011212739190674565)
XLA Ops:
  0.0 0.7 %slice.3 = bf16[16,256]{1,0:T(8,128)(2,1)S(1)} slice(bf16[512,256]{1,0:T(8,128)(2,1)} %tokens_hbm.1), slice={[496:512], [0:256]} | slice | bytes 16384 | tf_op jit(solution)/shard_map/slice | solution.py:273
  0.7 1.6 %collective-permute-start = (bf16[16,256]{1,0:T(8,128)(2,1)S(1)}, bf16[16,256]{1,0:T(8,128)(2,1)S(1)}, u32[]{:S(2)}, u32[]{:S(2)}) collective-permute-start(bf16[16,256]{1,0:T(8,128)(2,1)S(1)} %slice.3), channel_id=1, source_target_pairs={{0,1},{1,2},{2,3},{3,4},{4,5},{5,6},{6,7},{7,8},{8,9},{9,10},{10,1... | collective-permute-start | bytes 24584 | tf_op jit(solution)/shard_map/ppermute | solution.py:265
  2.3 0.1 pad_add_fusion.place_ref
  2.4 0.0 copy-done.7
  2.4 0.0 copy-start.5
  2.4 0.9 %copy-done.5 = bf16[512,256]{1,0:T(8,128)(2,1)S(1)} copy-done((bf16[512,256]{1,0:T(8,128)(2,1)S(1)}, bf16[512,256]{1,0:T(8,128)(2,1)}, u32[]{:S(2)}) %copy-start.5) | copy-done | bytes 262168
  3.3 0.0 copy-start.6
  3.3 1.0 %copy-done.6 = bf16[256,768]{1,0:T(8,128)(2,1)S(1)} copy-done((bf16[256,768]{1,0:T(8,128)(2,1)S(1)}, bf16[256,768]{1,0:T(8,128)(2,1)}, u32[]{:S(2)}) %copy-start.6) | copy-done | bytes 393240
  4.3 1.2 %project.1 = (bf16[256,512]{1,0:T(8,128)(2,1)S(1)}, f32[512,256]{1,0:T(8,128)S(1)}, f32[8,768]{1,0:T(8,128)S(1)}, bf16[256,768]{1,0:T(8,128)(2,1)S(1)}, f32[3,768]{1,0:T(4,128)S(1)}) custom-call(bf16[512,256]{1,0:T(8,128)(2,1)S(1)} %copy-done.5, bf16[256,768]{1,0:T(8,128)(2,1)S(1)} %copy-done.6, f32[3,768]{1,0:T(4,128)S(1)} %copy-done.7), custom_call_target="tpu_custom_call" | custom-call | flops 201326592 | bytes 2097152 | tf_op jit(solution)/shard_map/project/pallas_call | solution.py:78
  5.5 4.6 %collective-permute-done.rim_ref = bf16[16,256]{1,0:T(8,128)(2,1)S(1)} collective-permute-done((bf16[16,256]{1,0:T(8,128)(2,1)S(1)}, bf16[16,256]{1,0:T(8,128)(2,1)S(1)}, u32[]{:S(2)}, u32[]{:S(2)}) %collective-permute-start) | collective-permute-done | bytes 8224 | tf_op jit(solution)/shard_map/ppermute | solution.py:265
  10.0 0.8 %fix_rim.1 = (bf16[256,512]{1,0:T(8,128)(2,1)S(1)}, f32[8,256]{1,0:T(8,128)S(1)}) custom-call(s32[2]{0:T(128)S(1)} %pad_add_fusion.place_ref, bf16[16,256]{1,0:T(8,128)(2,1)S(1)} %collective-permute-done.rim_ref, bf16[256,768]{1,0:T(8,128)(2,1)S(1)} %get-tuple-element.12.w_ref, f32[3,768]{1,0:T(4,128)S(1)} %get-tuple-element.13.taps_ref, ...), custom_call_target="tpu_custom_call" | custom-call | flops 20000000 | bytes 1048576 | tf_op jit(solution)/shard_map/fix_rim/pallas_call | solution.py:116
  10.9 0.0 copy-start
  10.9 0.0 copy-start.2
  10.9 0.0 copy-start.3
  10.9 0.0 copy-start.4
  10.9 16.2 %all_to_all.10.own_ref = bf16[16,16,512]{2,1,0:T(8,128)(2,1)S(1)} all-to-all(bf16[16,16,512]{2,1,0:T(8,128)(2,1)S(1)} %bitcast.5), channel_id=1, replica_groups=mesh['span'=16,'tok'=16] {'tok'}, dimensions={0} | all-to-all | bytes 524288 | tf_op jit(solution)/shard_map/all_to_all | solution.py:276
  27.1 0.0 copy-start.8
  27.1 0.0 collective-permute-start.1
  27.1 0.0 copy-done
  27.1 0.0 copy-done.2
  27.1 0.0 copy-done.3
  27.1 0.0 copy-done.4
  27.1 0.5 %spectrum.1.spec_ref = f32[1024,256]{1,0:T(8,128)S(1)} custom-call(bf16[16,8192]{1,0:T(8,128)(2,1)S(1)} %copy-done, bf16[128,128]{1,0:T(8,128)(2,1)S(1)} %copy-done.4, bf16[256,256]{1,0:T(8,128)(2,1)S(1)} %copy-done.2, f32[2,64,128]{2,1,0:T(8,128)S(1)} %copy-done.3), custom_call_target="tpu_custom_call" | custom-call | flops 400000000 | bytes 3145728 | tf_op jit(solution)/shard_map/spectrum/pallas_call | solution.py:167
  27.7 7.6 %collective-permute-done.1.past_ref = bf16[16,16,512]{2,1,0:T(8,128)(2,1)S(1)} collective-permute-done((bf16[16,16,512]{2,1,0:T(8,128)(2,1)S(1)}, bf16[16,16,512]{2,1,0:T(8,128)(2,1)S(1)}, u32[]{:S(2)}, u32[]{:S(2)}) %collective-permute-start.1) | collective-permute-done | bytes 262176 | tf_op jit(solution)/shard_map/ppermute | solution.py:265
  35.3 0.0 copy-done.8
  35.3 0.0 copy-done.9
  35.3 0.0 copy-done.10
  35.3 1.7 %convolve.1 = bf16[16,16,512]{2,1,0:T(8,128)(2,1)S(1)} custom-call(s32[2]{0:T(128)S(1)} %pad_add_fusion.place_ref, bf16[16,16,512]{2,1,0:T(8,128)(2,1)S(1)} %collective-permute-done.1.past_ref, bf16[16,16,512]{2,1,0:T(8,128)(2,1)S(1)} %all_to_all.10.own_ref, f32[1024,256]{1,0:T(8,128)S(1)} %spectrum.1.spec_ref, f32[16]{0:T(128)S(1)} %copy-done.8, ...), custom_call_target="tpu_custom_call" | custom-call | flops 800000000 | bytes 4194304 | tf_op jit(solution)/shard_map/convolve/pallas_call | solution.py:229
  37.0 0.0 copy-start.1
  37.0 13.7 %all_to_all.11 = bf16[16,16,512]{2,1,0:T(8,128)(2,1)S(1)} all-to-all(bf16[16,16,512]{2,1,0:T(8,128)(2,1)S(1)} %convolve.1), channel_id=1, replica_groups=mesh['span'=16,'tok'=16] {'tok'}, dimensions={0} | all-to-all | bytes 524288 | tf_op jit(solution)/shard_map/all_to_all | solution.py:282
  50.7 0.0 copy-done.1
  50.7 1.0 %project_out.1 = bf16[512,256]{1,0:T(8,128)(2,1)} custom-call(bf16[256,512]{1,0:T(8,128)(2,1)S(1)} %bitcast.4, f32[512,256]{1,0:T(8,128)S(1)} %get-tuple-element.17.query_ref, f32[8,256]{1,0:T(8,128)S(1)} %get-tuple-element.18.head_ref, bf16[256,256]{1,0:T(8,128)(2,1)S(1)} %copy-done.1), custom_call_target="tpu_custom_call" | custom-call | flops 67108864 | bytes 2097152 | tf_op jit(solution)/shard_map/project_out/pallas_call | solution.py:252
  (3 shorter events, 0.0 us)
Async XLA Ops:
  0.7 1.7 %copy-start.7 = (f32[3,768]{1,0:T(4,128)S(1)}, f32[3,768]{1,0:T(4,128)}, u32[]{:S(2)}) copy-start(f32[3,768]{1,0:T(4,128)} %taps_hbm.1) | copy-start | bytes 27652
  0.7 9.3 %collective-permute-start = (bf16[16,256]{1,0:T(8,128)(2,1)S(1)}, bf16[16,256]{1,0:T(8,128)(2,1)S(1)}, u32[]{:S(2)}, u32[]{:S(2)}) collective-permute-start(bf16[16,256]{1,0:T(8,128)(2,1)S(1)} %slice.3), channel_id=1, source_target_pairs={{0,1},{1,2},{2,3},{3,4},{4,5},{5,6},{6,7},{7,8},{8,9},{9,10},{10,1... | collective-permute-start | bytes 24584 | tf_op jit(solution)/shard_map/ppermute | solution.py:265
  2.4 1.0 %copy-start.5 = (bf16[512,256]{1,0:T(8,128)(2,1)S(1)}, bf16[512,256]{1,0:T(8,128)(2,1)}, u32[]{:S(2)}) copy-start(bf16[512,256]{1,0:T(8,128)(2,1)} %tokens_hbm.1) | copy-start | bytes 786436
  3.3 1.0 %copy-start.6 = (bf16[256,768]{1,0:T(8,128)(2,1)S(1)}, bf16[256,768]{1,0:T(8,128)(2,1)}, u32[]{:S(2)}) copy-start(bf16[256,768]{1,0:T(8,128)(2,1)} %w_hbm.1) | copy-start | bytes 1179652
  10.9 16.2 %copy-start = (bf16[16,8192]{1,0:T(8,128)(2,1)S(1)}, bf16[16,8192]{1,0:T(8,128)(2,1)}, u32[]{:S(2)}) copy-start(bf16[16,8192]{1,0:T(8,128)(2,1)} %filter_ref.1) | copy-start | bytes 786436
  10.9 16.2 %copy-start.2 = (bf16[256,256]{1,0:T(8,128)(2,1)S(1)}, bf16[256,256]{1,0:T(8,128)(2,1)}, u32[]{:S(2)}) copy-start(bf16[256,256]{1,0:T(8,128)(2,1)} %constant.23.cols_in_ref) | copy-start | bytes 393220
  10.9 16.2 %copy-start.3 = (f32[2,64,128]{2,1,0:T(8,128)S(1)}, f32[2,64,128]{2,1,0:T(8,128)}, u32[]{:S(2)}) copy-start(f32[2,64,128]{2,1,0:T(8,128)} %constant.21.clone.twist_ref) | copy-start | bytes 196612
  10.9 16.2 %copy-start.4 = (bf16[128,128]{1,0:T(8,128)(2,1)S(1)}, bf16[128,128]{1,0:T(8,128)(2,1)}, u32[]{:S(2)}) copy-start(bf16[128,128]{1,0:T(8,128)(2,1)} %constant.22.into_ref) | copy-start | bytes 98308
  27.1 8.2 %copy-start.8 = (f32[16]{0:T(128)S(1)}, f32[16]{0:T(128)}, u32[]{:S(2)}) copy-start(f32[16]{0:T(128)} %gain_ref.1) | copy-start | bytes 196
  27.1 8.2 %copy-start.9 = (bf16[256,256]{1,0:T(8,128)(2,1)S(1)}, bf16[256,256]{1,0:T(8,128)(2,1)}, u32[]{:S(2)}) copy-start(bf16[256,256]{1,0:T(8,128)(2,1)} %constant.24.cols_out_ref) | copy-start | bytes 393220
  27.1 8.2 %copy-start.10 = (bf16[64,128]{1,0:T(8,128)(2,1)S(1)}, bf16[64,128]{1,0:T(8,128)(2,1)}, u32[]{:S(2)}) copy-start(bf16[64,128]{1,0:T(8,128)(2,1)} %constant.25.back_ref) | copy-start | bytes 49156
  27.1 8.2 %collective-permute-start.1 = (bf16[16,16,512]{2,1,0:T(8,128)(2,1)S(1)}, bf16[16,16,512]{2,1,0:T(8,128)(2,1)S(1)}, u32[]{:S(2)}, u32[]{:S(2)}) collective-permute-start(bf16[16,16,512]{2,1,0:T(8,128)(2,1)S(1)} %all_to_all.10.own_ref), channel_id=1, source_target_pairs={{0,16},{16,32},{32,48},{48,64},{64,80},{80,96},{96,112},{112,128},... | collective-permute-start | bytes 786440 | tf_op jit(solution)/shard_map/ppermute | solution.py:265
  37.0 13.8 %copy-start.1 = (bf16[256,256]{1,0:T(8,128)(2,1)S(1)}, bf16[256,256]{1,0:T(8,128)(2,1)}, u32[]{:S(2)}) copy-start(bf16[256,256]{1,0:T(8,128)(2,1)} %w_ref.1) | copy-start | bytes 393220

commit v3 on v2

v3 whole, which is shorter than its diff:
```python
import jax
import jax.numpy as jnp
import numpy as np
from jax import lax
from jax.experimental import pallas as pl
from jax.experimental.pallas import tpu as pltpu
from jax.sharding import PartitionSpec as P

D = 256
LANES = 128
HALF = 64
RIM = 16
POINTS = LANES * LANES


def dft_tables():
    ka = np.arange(HALF) + 0.5
    idx = np.arange(LANES)
    wave = lambda phase: np.exp(-2j * np.pi * phase)
    rows = wave(np.outer(ka, idx) / LANES)
    twist = wave(np.outer(ka, idx) / POINTS)
    cols = wave(np.outer(idx, idx) / LANES)
    into = np.concatenate([rows.real, rows.imag], 0)
    back = into.T[HALF:] * (2.0 / POINTS)
    cols_in = np.block([[cols.real, cols.imag], [-cols.imag, cols.real]])
    cols_out = np.block([[cols.real.T, -cols.imag.T], [cols.imag.T, cols.real.T]])
    bf = lambda a: a.astype(np.float32).astype(jnp.bfloat16)
    pair = lambda a: np.concatenate([bf(a), bf(a - bf(a).astype(np.float64))], 1)
    twist = np.stack([twist.real, twist.imag]).astype(np.float32)
    tables = pair(into[:, :HALF]), pair(into[:, HALF:]), bf(cols_in), bf(cols_out), pair(back), twist
    return [jnp.asarray(table) for table in tables]


def dot(a, b):
    return jnp.dot(a, b, preferred_element_type=jnp.float32)


VMEM = pl.BlockSpec(memory_space=pltpu.VMEM)
HBM = pl.BlockSpec(memory_space=pltpu.MemorySpace.HBM)
HEAD = 8
PIECES = 4


def short_filter_sum(taps, now, one, two):
    return taps[0:1] * now + taps[1:2] * one + taps[2:3] * two


def rounded(projected):
    return projected.astype(jnp.bfloat16).astype(jnp.float32)


def project_kernel(
    tokens_hbm, w_hbm, taps_hbm, product_ref, head_ref, w_ref, taps_ref, tokens_ref, sems
):
    copies = [
        pltpu.make_async_copy(w_hbm.at[:, pl.ds(D, 2 * D)], w_ref, sems.at[0]),
        pltpu.make_async_copy(tokens_hbm, tokens_ref, sems.at[1]),
        pltpu.make_async_copy(taps_hbm, taps_ref, sems.at[2]),
    ]
    for copy in copies:
        copy.start()
    for copy in copies:
        copy.wait()

    def mixed(part):
        cols = slice(part * D, (part + 1) * D)
        now = rounded(dot(tokens_ref[...], w_ref[:, cols]))
        head_ref[:, cols] = now[:HEAD]
        taps = taps_ref[:, (part + 1) * D : (part + 2) * D]
        return short_filter_sum(taps, now, pltpu.roll(now, 1, axis=0), pltpu.roll(now, 2, axis=0))

    product = mixed(0) * mixed(1)
    product_ref[...] = jnp.transpose(product, (1, 0)).astype(jnp.bfloat16)


def project(tokens, w_in, short_filter):
    rows = tokens.shape[0]
    inputs = [
        pltpu.with_memory_space_constraint(a, pltpu.MemorySpace.HBM)
        for a in (tokens, w_in, short_filter)
    ]
    return pl.pallas_call(
        project_kernel,
        out_shape=(
            jax.ShapeDtypeStruct((D, rows), jnp.bfloat16),
            jax.ShapeDtypeStruct((HEAD, 2 * D), jnp.float32),
            jax.ShapeDtypeStruct((D, 2 * D), w_in.dtype),
            jax.ShapeDtypeStruct(short_filter.shape, short_filter.dtype),
        ),
        in_specs=[HBM] * 3,
        out_specs=(VMEM,) * 4,
        scratch_shapes=[pltpu.VMEM(tokens.shape, tokens.dtype), pltpu.SemaphoreType.DMA((3,))],
        compiler_params=pltpu.CompilerParams(vmem_limit_bytes=24 << 20),
        cost_estimate=pl.CostEstimate(
            flops=2 * rows * D * 2 * D, bytes_accessed=2 << 20, transcendentals=0
        ),
        name="project",
    )(*inputs)


def rim_kernel(there_ref, rim_ref, w_ref, taps_ref, head_ref, raw_ref, product_ref):
    before = rounded(dot(rim_ref[...], w_ref[...]))[RIM - HEAD :]
    there = jnp.concatenate([there_ref[0:1], there_ref[0:1]], axis=1)
    before = jnp.where(there > 0.0, before, 0.0)
    both = jnp.concatenate([before, head_ref[...]], axis=0)
    mixed = short_filter_sum(
        taps_ref[:, D:], both, pltpu.roll(both, 1, axis=0), pltpu.roll(both, 2, axis=0)
    )[HEAD:]
    fixed = mixed[:, :D] * mixed[:, D:]
    fixed = jnp.concatenate([fixed, jnp.zeros((LANES - HEAD, D), jnp.float32)], axis=0)
    fixed = jnp.transpose(fixed, (1, 0)).astype(jnp.bfloat16)
    lane = lax.broadcasted_iota(jnp.int32, fixed.shape, 1)
    product_ref[:, LANES:] = raw_ref[:, LANES:]
    product_ref[:, :LANES] = jnp.where(lane < HEAD, fixed, raw_ref[:, :LANES])


def fix_rim(there, rim, w_part, short_filter, head, product):
    return pl.pallas_call(
        rim_kernel,
        out_shape=jax.ShapeDtypeStruct(product.shape, product.dtype),
        in_specs=[VMEM] * 6,
        out_specs=VMEM,
        compiler_params=pltpu.CompilerParams(vmem_limit_bytes=16 << 20),
        cost_estimate=pl.CostEstimate(flops=20_000_000, bytes_accessed=1 << 20, transcendentals=0),
        name="fix_rim",
    )(there, rim, w_part, short_filter, head, product)


def query_kernel(there_ref, tokens_ref, rim_ref, w_ref, taps_ref, query_ref):
    weights = w_ref[:, :D]
    taps = taps_ref[:, :D]
    now = rounded(dot(tokens_ref[...], weights))
    query_ref[...] = short_filter_sum(
        taps, now, pltpu.roll(now, 1, axis=0), pltpu.roll(now, 2, axis=0)
    )
    before = rounded(dot(rim_ref[...], weights))[RIM - HEAD :]
    both = jnp.concatenate([jnp.where(there_ref[0:1] > 0.0, before, 0.0), now[:HEAD]], axis=0)
    query_ref[:HEAD] = short_filter_sum(
        taps, both, pltpu.roll(both, 1, axis=0), pltpu.roll(both, 2, axis=0)
    )[HEAD:]


def make_query(there, tokens, rim, w_in, short_filter):
    rows = tokens.shape[0]
    return pl.pallas_call(
        query_kernel,
        out_shape=jax.ShapeDtypeStruct((rows, D), jnp.float32),
        in_specs=[VMEM] * 5,
        out_specs=VMEM,
        compiler_params=pltpu.CompilerParams(vmem_limit_bytes=16 << 20),
        cost_estimate=pl.CostEstimate(
            flops=2 * rows * D * D, bytes_accessed=1 << 20, transcendentals=0
        ),
        name="make_query",
    )(there, tokens, rim, w_in, short_filter)


def put_rows(load, scratch, chans, tiles, at):
    for tile in range(tiles):
        scratch[pl.ds((at + tile) * chans, chans), :] = load(tile).astype(jnp.float32)


def by_channel(scratch, chans, at, tiles):
    return jnp.concatenate(
        [scratch[pl.ds(at * chans + c, tiles, stride=chans), :] for c in range(chans)], axis=1
    )


def forward(into, cols_in, twist_re, twist_im, data, chans):
    first = dot(into, jnp.concatenate([data, data], axis=0))
    spun = []
    for c in range(chans):
        re = first[:HALF, c * LANES : (c + 1) * LANES]
        im = first[HALF:, c * LANES : (c + 1) * LANES]
        spun.append(
            jnp.concatenate(
                [re * twist_re - im * twist_im, re * twist_im + im * twist_re], axis=1
            ).astype(jnp.bfloat16)
        )
    return dot(jnp.concatenate(spun, axis=0), cols_in)


def rows_of(ref):
    per = ref.shape[2] // LANES
    return lambda i: ref[i // per, :, (i % per) * LANES : (i % per + 1) * LANES]


def early_kernel(
    filter_ref, own_ref, gain_ref, into_lo_ref, into_hi_ref, cols_in_ref, twist_ref, spec_ref,
    freq_ref, skip_ref, rows_ref,
):
    chans, taps = filter_ref.shape
    tiles = taps // LANES
    put_rows(lambda i: filter_ref[:, i * LANES : (i + 1) * LANES], rows_ref, chans, tiles, 0)
    gain = jnp.broadcast_to(gain_ref[...], (chans, LANES))
    per = own_ref.shape[2] // LANES
    for tile in range(tiles):
        lanes = slice(tile % per * LANES, (tile % per + 1) * LANES)
        own = own_ref[tile // per, :, lanes].astype(jnp.float32)
        rows_ref[pl.ds((tiles + tile) * chans, chans), :] = own
        skip_ref[tile // per, :, lanes] = gain * own
    twist = twist_ref[0], twist_ref[1]
    data = by_channel(rows_ref, chans, 0, tiles).astype(jnp.bfloat16)
    spec_ref[...] = forward(into_lo_ref[...], cols_in_ref[...], *twist, data, chans)
    data = by_channel(rows_ref, chans, tiles, tiles)
    freq_ref[...] = forward(
        into_hi_ref[...], cols_in_ref[...], *twist, data.astype(jnp.bfloat16), chans
    )


def early(long_filter, own, gain, into_lo, into_hi, cols_in, twist):
    chans, taps = long_filter.shape
    tiles = taps // LANES
    points = jax.ShapeDtypeStruct((chans * HALF, 2 * LANES), jnp.float32)
    return pl.pallas_call(
        early_kernel,
        out_shape=(points, points, jax.ShapeDtypeStruct(own.shape, jnp.float32)),
        in_specs=[VMEM] * 7,
        out_specs=(VMEM,) * 3,
        scratch_shapes=[pltpu.VMEM((2 * tiles * chans, LANES), jnp.float32)],
        compiler_params=pltpu.CompilerParams(vmem_limit_bytes=24 << 20),
        cost_estimate=pl.CostEstimate(
            flops=800_000_000, bytes_accessed=3 << 20, transcendentals=0
        ),
        name="early",
    )(long_filter, own, gain, into_lo, into_hi, cols_in, twist)


def convolve_kernel(
    there_ref, past_ref, spec_ref, freq_ref, skip_ref, into_lo_ref, cols_in_ref, cols_out_ref,
    back_ref, twist_ref, out_ref, rows_ref,
):
    peers, chans, width = out_ref.shape
    per = width // LANES
    tiles = peers * per
    twist_re = twist_ref[0]
    twist_im = twist_ref[1]
    there = jnp.broadcast_to(there_ref[1:2, :LANES], (chans, LANES)) > 0.0
    load = rows_of(past_ref)
    put_rows(lambda i: jnp.where(there, load(i).astype(jnp.float32), 0.0), rows_ref, chans, tiles, 0)
    past = by_channel(rows_ref, chans, 0, tiles).astype(jnp.bfloat16)
    freq = forward(into_lo_ref[...], cols_in_ref[...], twist_re, twist_im, past, chans) + freq_ref[...]
    spec = spec_ref[...]
    fre, fim = freq[:, :LANES], freq[:, LANES:]
    sre, sim = spec[:, :LANES], spec[:, LANES:]
    prod = jnp.concatenate([fre * sre - fim * sim, fre * sim + fim * sre], axis=1)
    last = dot(prod.astype(jnp.bfloat16), cols_out_ref[...])
    spun = []
    for c in range(chans):
        re = last[c * HALF : (c + 1) * HALF, :LANES]
        im = last[c * HALF : (c + 1) * HALF, LANES:]
        spun.append(
            jnp.concatenate(
                [re * twist_re + im * twist_im, im * twist_re - re * twist_im], axis=0
            ).astype(jnp.bfloat16)
        )
    spun = jnp.concatenate(spun, axis=1)
    result = dot(back_ref[...], jnp.concatenate([spun, spun], axis=0))
    for c in range(chans):
        lanes = slice(c * LANES, (c + 1) * LANES)
        rows_ref[pl.ds(c, tiles, stride=chans), :] = result[:, lanes]
    for tile in range(tiles):
        lanes = slice(tile % per * LANES, (tile % per + 1) * LANES)
        out = rows_ref[pl.ds(tile * chans, chans), :] + skip_ref[tile // per, :, lanes]
        out_ref[tile // per, :, lanes] = out.astype(jnp.bfloat16)


def convolve(there, past, spec, freq, skip, into_lo, cols_in, cols_out, back, twist):
    peers, chans, width = past.shape
    return pl.pallas_call(
        convolve_kernel,
        out_shape=jax.ShapeDtypeStruct(past.shape, jnp.bfloat16),
        in_specs=[VMEM] * 10,
        out_specs=VMEM,
        scratch_shapes=[pltpu.VMEM((peers * chans * width // LANES, LANES), jnp.float32)],
        compiler_params=pltpu.CompilerParams(vmem_limit_bytes=32 << 20),
        cost_estimate=pl.CostEstimate(
            flops=800_000_000, bytes_accessed=4 << 20, transcendentals=0
        ),
        name="convolve",
    )(there, past, spec, freq, skip, into_lo, cols_in, cols_out, back, twist)


def output_kernel(conv_ref, query_ref, w_ref, out_hbm, out_ref, sems):
    rows = query_ref.shape[0] // PIECES
    copies = []
    for piece in range(PIECES):
        at = slice(piece * rows, (piece + 1) * rows)
        conv = jnp.transpose(conv_ref[:, at].astype(jnp.float32), (1, 0))
        gated = (query_ref[at] * conv).astype(jnp.bfloat16)
        out_ref[at] = dot(gated, w_ref[...]).astype(jnp.bfloat16)
        copies.append(pltpu.make_async_copy(out_ref.at[at], out_hbm.at[at], sems.at[piece]))
        copies[-1].start()
    for copy in copies:
        copy.wait()


def project_out(conv, query, w_out):
    rows = query.shape[0]
    return pl.pallas_call(
        output_kernel,
        out_shape=jax.ShapeDtypeStruct((rows, D), jnp.bfloat16),
        in_specs=[VMEM] * 3,
        out_specs=HBM,
        scratch_shapes=[
            pltpu.VMEM((rows, D), jnp.bfloat16), pltpu.SemaphoreType.DMA((PIECES,))
        ],
        compiler_params=pltpu.CompilerParams(vmem_limit_bytes=16 << 20),
        cost_estimate=pl.CostEstimate(
            flops=2 * rows * D * D, bytes_accessed=2 << 20, transcendentals=0
        ),
        name="project_out",
    )(conv, query, w_out)


def rotated(array, axes):
    count = lax.axis_size(axes)
    return lax.ppermute(array, axes, [(i, (i + 1) % count) for i in range(count)])


def per_device(tokens, w_in, short_filter, long_filter, skip_gain, w_out):
    rows = tokens.shape[0]
    peers = lax.axis_size("tok")
    into_lo, into_hi, cols_in, cols_out, back, twist = dft_tables()
    span = lax.axis_index("span")
    there = jnp.stack([span + lax.axis_index("tok") > 0, span > 0]).astype(jnp.float32)
    there = jnp.broadcast_to(there[:, None], (2, D))
    rim = rotated(tokens[rows - RIM :], ("span", "tok"))
    product, head, w_part, taps = project(tokens, w_in, short_filter)
    product = fix_rim(there, rim, w_part, taps, head, product)
    own = lax.all_to_all(
        product.reshape(peers, D // peers, rows), "tok", split_axis=0, concat_axis=0, tiled=True
    )
    past = rotated(own, "span")
    spec, freq, skip = early(long_filter, own, skip_gain.reshape(-1, 1), into_lo, into_hi, cols_in, twist)
    query = make_query(there, tokens, rim, w_in, short_filter)
    freq, query = lax.optimization_barrier((freq, query))
    conv = convolve(there, past, spec, freq, skip, into_lo, cols_in, cols_out, back, twist)
    conv = lax.all_to_all(conv, "tok", split_axis=0, concat_axis=0, tiled=True)
    return project_out(conv.reshape(D, rows), query, w_out)


def solution(mesh):
    return jax.shard_map(
        per_device,
        mesh=mesh,
        in_specs=(P(("span", "tok"), None), P(), P(), P("tok", None), P("tok"), P()),
        out_specs=P(("span", "tok"), None),
        check_vma=False,
    )
```

time: 52 us -> 50.5 us (0.971)
  waiting for transfers between devices: 12.2 us -> 11.3 us
    ppermute x2, waiting for transfers between devices: 12.2 us -> 11.3 us  [rotated(): lax.ppermute(array, axes, [(i, (i + 1) % count) for i in range(count)])]
    unnamed x22 -> x24, local copies, waits for them, and re-layouts: 1.99 us -> 1.37 us
    pallas_call x1, Pallas kernels: 1.16 us -> 1.76 us  [project(): pl.pallas_call(project_kernel, out_shape=(jax.ShapeDtypeStruct((D, rows),...]
    pallas_call x3 -> x4, Pallas kernels: 3.05 us -> 2.58 us  [the longest x1 0.99 us: convolve(): pl.pallas_call(convolve_kernel, out_shape=jax.ShapeDtypeStruct(past.shape...]
  transfers between devices with their start and end apart: 2 -> 2, of which waited for: 2 -> 2; matrix products, arithmetic and copies ran while one was open for 0% -> 0% of each run, Pallas kernels for 3% -> 6%
where the time goes in v3:
time: 50.5 us; the launch traced here: 50.3 us
  blocking collectives  29.7 us (59%)
  waiting for transfers between devices  11.3 us (22%)
  Pallas kernels  5.31 us (11%)
  local copies, waits for them, and re-layouts  2.22 us (4%)
  starting transfers between devices  1.58 us (3%)
    all_to_all x1, blocking collectives, per_device(): lax.all_to_all(product.reshape(peers, D // peers, rows), 'tok', split_axi...  15.9 us
    all_to_all x1, blocking collectives, per_device(): conv = lax.all_to_all(conv, 'tok', split_axis=0, concat_axis=0, tiled=True)  13.7 us
    ppermute x2, waiting for transfers between devices, rotated(): lax.ppermute(array, axes, [(i, (i + 1) % count) for i in range(count)])  11.3 us
    pallas_call x1, Pallas kernels, project(): pl.pallas_call(project_kernel, out_shape=(jax.ShapeDtypeStruct((D, rows),...  1.76 us
    ppermute x2, starting transfers between devices, rotated(): lax.ppermute(array, axes, [(i, (i + 1) % count) for i in range(count)])  1.58 us
    unnamed x24, local copies, waits for them, and re-layouts  1.37 us
  transfers between devices with their start and end apart: 2, of which 2 were waited for; matrix products, arithmetic and copies ran while one was open for 0% of the time, Pallas kernels for 6%

profile of v3, /device:TPU:6, one launch (start us, length us, event | category | flops | bytes accessed | tf_op | source)
XLA Modules:
  0.0 50.3 jit_solution(1752346691286228534)
XLA Ops:
  0.0 0.7 %slice.3 = bf16[16,256]{1,0:T(8,128)(2,1)S(1)} slice(bf16[512,256]{1,0:T(8,128)(2,1)} %tokens_ref.1), slice={[496:512], [0:256]} | slice | bytes 16384 | tf_op jit(solution)/shard_map/slice | solution.py:328
  0.7 1.6 %collective-permute-start = (bf16[16,256]{1,0:T(8,128)(2,1)S(1)}, bf16[16,256]{1,0:T(8,128)(2,1)S(1)}, u32[]{:S(2)}, u32[]{:S(2)}) collective-permute-start(bf16[16,256]{1,0:T(8,128)(2,1)S(1)} %slice.3), channel_id=1, source_target_pairs={{0,1},{1,2},{2,3},{3,4},{4,5},{5,6},{6,7},{7,8},{8,9},{9,10},{10,1... | collective-permute-start | bytes 24584 | tf_op jit(solution)/shard_map/ppermute | solution.py:318
  2.3 0.1 add_convert_fusion
  2.4 1.8 %project.1 = (bf16[256,512]{1,0:T(8,128)(2,1)S(1)}, f32[8,512]{1,0:T(8,128)S(1)}, bf16[256,512]{1,0:T(8,128)(2,1)S(1)}, f32[3,768]{1,0:T(4,128)S(1)}) custom-call(bf16[512,256]{1,0:T(8,128)(2,1)} %tokens_ref.1, bf16[256,768]{1,0:T(8,128)(2,1)} %w_ref.2, f32[3,768]{1,0:T(4,128)} %taps_ref.1), custom_call_target="tpu_custom_call" | custom-call | flops 134217728 | bytes 2097152 | tf_op jit(solution)/shard_map/project/pallas_call | solution.py:82
  4.1 5.9 %collective-permute-done.rim_ref = bf16[16,256]{1,0:T(8,128)(2,1)S(1)} collective-permute-done((bf16[16,256]{1,0:T(8,128)(2,1)S(1)}, bf16[16,256]{1,0:T(8,128)(2,1)S(1)}, u32[]{:S(2)}, u32[]{:S(2)}) %collective-permute-start) | collective-permute-done | bytes 8224 | tf_op jit(solution)/shard_map/ppermute | solution.py:318
  10.0 0.1 broadcast_in_dim.2.there_ref
  10.1 0.3 fix_rim.1
  10.4 0.0 copy-start
  10.4 0.0 copy-start.6
  10.4 15.9 %all_to_all.10.own_ref = bf16[16,16,512]{2,1,0:T(8,128)(2,1)S(1)} all-to-all(bf16[16,16,512]{2,1,0:T(8,128)(2,1)S(1)} %bitcast.5), channel_id=1, replica_groups=mesh['span'=16,'tok'=16] {'tok'}, dimensions={0} | all-to-all | bytes 524288 | tf_op jit(solution)/shard_map/all_to_all | solution.py:331
  26.3 0.0 collective-permute-start.1
  26.3 0.7 %copy-done.11 = f32[16]{0:T(128)S(1)} copy-done((f32[16]{0:T(128)S(1)}, f32[16]{0:T(128)}, u32[]{:S(2)}) %copy-start.11) | copy-done | bytes 88
  27.0 0.1 copy.13.gain_ref
  27.1 0.0 copy-done.1
  27.1 0.0 copy-done
  27.1 0.0 copy-done.6
  27.1 0.0 copy-start.3
  27.1 0.0 copy-start.5
  27.1 0.0 copy-start.7
  27.1 0.0 copy-start.9
  27.1 0.0 copy-start.10
  27.1 0.4 make_query.1.query_ref
  27.5 0.5 copy-done.3
  28.0 0.2 copy-done.9
  28.2 0.0 copy-done.10
  28.2 1.0 %early.1 = (f32[1024,256]{1,0:T(8,128)S(1)}, f32[1024,256]{1,0:T(8,128)S(1)}, f32[16,16,512]{2,1,0:T(8,128)S(1)}) custom-call(bf16[16,8192]{1,0:T(8,128)(2,1)S(1)} %copy-done.9, bf16[16,16,512]{2,1,0:T(8,128)(2,1)S(1)} %all_to_all.10.own_ref, f32[16,1]{1,0:T(8,128)S(1)} %copy.13.gain_ref, bf16[128,128]{1,0:T(8,128)(2,1)S(1)} %copy-done.7, ...), custom_call_target="tpu_custom_call" | custom-call | flops 800000000 | bytes 3145728 | tf_op jit(solution)/shard_map/early/pallas_call | solution.py:215
  29.1 5.4 %collective-permute-done.1.past_ref = bf16[16,16,512]{2,1,0:T(8,128)(2,1)S(1)} collective-permute-done((bf16[16,16,512]{2,1,0:T(8,128)(2,1)S(1)}, bf16[16,16,512]{2,1,0:T(8,128)(2,1)S(1)}, u32[]{:S(2)}, u32[]{:S(2)}) %collective-permute-start.1) | collective-permute-done | bytes 262176 | tf_op jit(solution)/shard_map/ppermute | solution.py:318
  34.5 0.0 copy-done.4
  34.5 1.0 %convolve.1 = bf16[16,16,512]{2,1,0:T(8,128)(2,1)S(1)} custom-call(f32[2,256]{1,0:T(2,128)S(1)} %broadcast_in_dim.2.there_ref, bf16[16,16,512]{2,1,0:T(8,128)(2,1)S(1)} %collective-permute-done.1.past_ref, f32[1024,256]{1,0:T(8,128)S(1)} %get-tuple-element.18.spec_ref, f32[1024,256]{1,0:T(8,128)S(1)} %get-tuple-element.20.freq_ref, ...), custom_call_target="tpu_custom_call" | custom-call | flops 800000000 | bytes 4194304 | tf_op jit(solution)/shard_map/convolve/pallas_call | solution.py:270
  35.5 0.0 copy-start.2
  35.5 13.7 %all_to_all.11 = bf16[16,16,512]{2,1,0:T(8,128)(2,1)S(1)} all-to-all(bf16[16,16,512]{2,1,0:T(8,128)(2,1)S(1)} %convolve.1), channel_id=1, replica_groups=mesh['span'=16,'tok'=16] {'tok'}, dimensions={0} | all-to-all | bytes 524288 | tf_op jit(solution)/shard_map/all_to_all | solution.py:339
  49.3 1.0 %project_out.1 = bf16[512,256]{1,0:T(8,128)(2,1)} custom-call(bf16[256,512]{1,0:T(8,128)(2,1)S(1)} %bitcast.6, f32[512,256]{1,0:T(8,128)S(1)} %make_query.1.query_ref, bf16[256,256]{1,0:T(8,128)(2,1)S(1)} %copy-done.2), custom_call_target="tpu_custom_call" | custom-call | flops 67108864 | bytes 2097152 | tf_op jit(solution)/shard_map/project_out/pallas_call | solution.py:300
  (8 shorter events, 0.0 us)
Async XLA Ops:
  0.7 9.3 %collective-permute-start = (bf16[16,256]{1,0:T(8,128)(2,1)S(1)}, bf16[16,256]{1,0:T(8,128)(2,1)S(1)}, u32[]{:S(2)}, u32[]{:S(2)}) collective-permute-start(bf16[16,256]{1,0:T(8,128)(2,1)S(1)} %slice.3), channel_id=1, source_target_pairs={{0,1},{1,2},{2,3},{3,4},{4,5},{5,6},{6,7},{7,8},{8,9},{9,10},{10,1... | collective-permute-start | bytes 24584 | tf_op jit(solution)/shard_map/ppermute | solution.py:318
  10.1 17.0 %copy-start.1 = (bf16[512,256]{1,0:T(8,128)(2,1)S(1)}, bf16[512,256]{1,0:T(8,128)(2,1)}, u32[]{:S(2)}) copy-start(bf16[512,256]{1,0:T(8,128)(2,1)} %tokens_ref.1) | copy-start | bytes 786436
  10.4 16.7 %copy-start = (bf16[256,768]{1,0:T(8,128)(2,1)S(1)}, bf16[256,768]{1,0:T(8,128)(2,1)}, u32[]{:S(2)}) copy-start(bf16[256,768]{1,0:T(8,128)(2,1)} %w_ref.2) | copy-start | bytes 1179652
  10.4 16.7 %copy-start.6 = (f32[3,768]{1,0:T(4,128)S(1)}, f32[3,768]{1,0:T(4,128)}, u32[]{:S(2)}) copy-start(f32[3,768]{1,0:T(4,128)} %taps_ref.1) | copy-start | bytes 27652
  26.3 0.7 %copy-start.11 = (f32[16]{0:T(128)S(1)}, f32[16]{0:T(128)}, u32[]{:S(2)}) copy-start(f32[16]{0:T(128)} %param.16) | copy-start | bytes 196
  26.3 8.2 %collective-permute-start.1 = (bf16[16,16,512]{2,1,0:T(8,128)(2,1)S(1)}, bf16[16,16,512]{2,1,0:T(8,128)(2,1)S(1)}, u32[]{:S(2)}, u32[]{:S(2)}) collective-permute-start(bf16[16,16,512]{2,1,0:T(8,128)(2,1)S(1)} %all_to_all.10.own_ref), channel_id=1, source_target_pairs={{0,16},{16,32},{32,48},{48,64},{64,80},{80,96},{96,112},{112,128},... | collective-permute-start | bytes 786440 | tf_op jit(solution)/shard_map/ppermute | solution.py:318
  27.1 0.9 %copy-start.3 = (bf16[256,256]{1,0:T(8,128)(2,1)S(1)}, bf16[256,256]{1,0:T(8,128)(2,1)}, u32[]{:S(2)}) copy-start(bf16[256,256]{1,0:T(8,128)(2,1)} %constant.23.clone.cols_in_ref) | copy-start | bytes 393220
  27.1 0.9 %copy-start.5 = (f32[2,64,128]{2,1,0:T(8,128)S(1)}, f32[2,64,128]{2,1,0:T(8,128)}, u32[]{:S(2)}) copy-start(f32[2,64,128]{2,1,0:T(8,128)} %constant.26.clone.twist_ref) | copy-start | bytes 196612
  27.1 0.9 %copy-start.7 = (bf16[128,128]{1,0:T(8,128)(2,1)S(1)}, bf16[128,128]{1,0:T(8,128)(2,1)}, u32[]{:S(2)}) copy-start(bf16[128,128]{1,0:T(8,128)(2,1)} %constant.21.clone.into_lo_ref) | copy-start | bytes 98308
  27.1 1.1 %copy-start.9 = (bf16[16,8192]{1,0:T(8,128)(2,1)S(1)}, bf16[16,8192]{1,0:T(8,128)(2,1)}, u32[]{:S(2)}) copy-start(bf16[16,8192]{1,0:T(8,128)(2,1)} %filter_ref.1) | copy-start | bytes 786436
  27.1 1.0 %copy-start.10 = (bf16[128,128]{1,0:T(8,128)(2,1)S(1)}, bf16[128,128]{1,0:T(8,128)(2,1)}, u32[]{:S(2)}) copy-start(bf16[128,128]{1,0:T(8,128)(2,1)} %constant.22.clone.into_hi_ref) | copy-start | bytes 98308
  28.2 6.4 %copy-start.4 = (bf16[256,256]{1,0:T(8,128)(2,1)S(1)}, bf16[256,256]{1,0:T(8,128)(2,1)}, u32[]{:S(2)}) copy-start(bf16[256,256]{1,0:T(8,128)(2,1)} %constant.24.clone.cols_out_ref) | copy-start | bytes 393220
  28.2 6.4 %copy-start.8 = (bf16[64,256]{1,0:T(8,128)(2,1)S(1)}, bf16[64,256]{1,0:T(8,128)(2,1)}, u32[]{:S(2)}) copy-start(bf16[64,256]{1,0:T(8,128)(2,1)} %constant.25.clone.back_ref) | copy-start | bytes 98308
  35.5 13.8 %copy-start.2 = (bf16[256,256]{1,0:T(8,128)(2,1)S(1)}, bf16[256,256]{1,0:T(8,128)(2,1)}, u32[]{:S(2)}) copy-start(bf16[256,256]{1,0:T(8,128)(2,1)} %w_ref.3) | copy-start | bytes 393220

commit v4 on v3

--- a/solution.py
+++ b/solution.py
@@ -27,7 +27,9 @@
     bf = lambda a: a.astype(np.float32).astype(jnp.bfloat16)
     pair = lambda a: np.concatenate([bf(a), bf(a - bf(a).astype(np.float64))], 1)
     twist = np.stack([twist.real, twist.imag]).astype(np.float32)
-    tables = pair(into[:, :HALF]), pair(into[:, HALF:]), bf(cols_in), bf(cols_out), pair(back), twist
+    high = bf(cols_in)
+    wide = np.concatenate([high, bf(cols_in - high.astype(np.float64)), high], 0)
+    tables = pair(into[:, :HALF]), pair(into[:, HALF:]), high, wide, bf(cols_out), pair(back), twist
     return [jnp.asarray(table) for table in tables]
 
 
@@ -38,7 +40,7 @@
 VMEM = pl.BlockSpec(memory_space=pltpu.VMEM)
 HBM = pl.BlockSpec(memory_space=pltpu.MemorySpace.HBM)
 HEAD = 8
-PIECES = 4
+PIECES = 2
 
 
 def short_filter_sum(taps, now, one, two):
@@ -62,14 +64,12 @@
     for copy in copies:
         copy.wait()
 
-    def mixed(part):
-        cols = slice(part * D, (part + 1) * D)
-        now = rounded(dot(tokens_ref[...], w_ref[:, cols]))
-        head_ref[:, cols] = now[:HEAD]
-        taps = taps_ref[:, (part + 1) * D : (part + 2) * D]
-        return short_filter_sum(taps, now, pltpu.roll(now, 1, axis=0), pltpu.roll(now, 2, axis=0))
-
-    product = mixed(0) * mixed(1)
+    now = rounded(dot(tokens_ref[...], w_ref[...]))
+    head_ref[...] = now[:HEAD]
+    mixed = short_filter_sum(
+        taps_ref[:, D:], now, pltpu.roll(now, 1, axis=0), pltpu.roll(now, 2, axis=0)
+    )
+    product = mixed[:, :D] * mixed[:, D:]
     product_ref[...] = jnp.transpose(product, (1, 0)).astype(jnp.bfloat16)
 
 
@@ -167,16 +167,20 @@
 
 
 def forward(into, cols_in, twist_re, twist_im, data, chans):
+    parts = cols_in.shape[0] // (2 * LANES)
     first = dot(into, jnp.concatenate([data, data], axis=0))
     spun = []
     for c in range(chans):
         re = first[:HALF, c * LANES : (c + 1) * LANES]
         im = first[HALF:, c * LANES : (c + 1) * LANES]
-        spun.append(
-            jnp.concatenate(
-                [re * twist_re - im * twist_im, re * twist_im + im * twist_re], axis=1
-            ).astype(jnp.bfloat16)
+        turned = jnp.concatenate(
+            [re * twist_re - im * twist_im, re * twist_im + im * twist_re], axis=1
         )
+        high = turned.astype(jnp.bfloat16)
+        row = [high] * min(parts, 2)
+        if parts == 3:
+            row.append((turned - high.astype(jnp.float32)).astype(jnp.bfloat16))
+        spun.append(jnp.concatenate(row, axis=1) if parts > 1 else high)
     return dot(jnp.concatenate(spun, axis=0), cols_in)
 
 
@@ -204,7 +208,7 @@
     spec_ref[...] = forward(into_lo_ref[...], cols_in_ref[...], *twist, data, chans)
     data = by_channel(rows_ref, chans, tiles, tiles)
     freq_ref[...] = forward(
-        into_hi_ref[...], cols_in_ref[...], *twist, data.astype(jnp.bfloat16), chans
+        into_hi_ref[...], cols_in_ref[: 4 * LANES], *twist, data.astype(jnp.bfloat16), chans
     )
 
 
@@ -321,7 +325,7 @@
 def per_device(tokens, w_in, short_filter, long_filter, skip_gain, w_out):
     rows = tokens.shape[0]
     peers = lax.axis_size("tok")
-    into_lo, into_hi, cols_in, cols_out, back, twist = dft_tables()
+    into_lo, into_hi, cols_in, cols_wide, cols_out, back, twist = dft_tables()
     span = lax.axis_index("span")
     there = jnp.stack([span + lax.axis_index("tok") > 0, span > 0]).astype(jnp.float32)
     there = jnp.broadcast_to(there[:, None], (2, D))
@@ -332,7 +336,7 @@
         product.reshape(peers, D // peers, rows), "tok", split_axis=0, concat_axis=0, tiled=True
     )
     past = rotated(own, "span")
-    spec, freq, skip = early(long_filter, own, skip_gain.reshape(-1, 1), into_lo, into_hi, cols_in, twist)
+    spec, freq, skip = early(long_filter, own, skip_gain.reshape(-1, 1), into_lo, into_hi, cols_wide, twist)
     query = make_query(there, tokens, rim, w_in, short_filter)
     freq, query = lax.optimization_barrier((freq, query))
     conv = convolve(there, past, spec, freq, skip, into_lo, cols_in, cols_out, back, twist)

time: 50.5 us -> 50.5 us (level)
    unnamed x24 -> x26, local copies, waits for them, and re-layouts: 1.37 us -> 1.42 us
  transfers between devices with their start and end apart: 2 -> 2, of which waited for: 2 -> 2; matrix products, arithmetic and copies ran while one was open for 0% -> 0% of each run, Pallas kernels for 6% -> 7%
where the time goes in v4:
time: 50.5 us; the launch traced here: 50.3 us
  blocking collectives  29.7 us (59%)
  waiting for transfers between devices  10.8 us (21%)
  Pallas kernels  5.75 us (11%)
  local copies, waits for them, and re-layouts  2.27 us (4%)
  starting transfers between devices  1.58 us (3%)
    all_to_all x1, blocking collectives, per_device(): lax.all_to_all(product.reshape(peers, D // peers, rows), 'tok', split_axi...  15.9 us
    all_to_all x1, blocking collectives, per_device(): conv = lax.all_to_all(conv, 'tok', split_axis=0, concat_axis=0, tiled=True)  13.7 us
    ppermute x2, waiting for transfers between devices, rotated(): lax.ppermute(array, axes, [(i, (i + 1) % count) for i in range(count)])  10.8 us
    pallas_call x1, Pallas kernels, project(): pl.pallas_call(project_kernel, out_shape=(jax.ShapeDtypeStruct((D, rows),...  1.75 us
    ppermute x2, starting transfers between devices, rotated(): lax.ppermute(array, axes, [(i, (i + 1) % count) for i in range(count)])  1.58 us
    unnamed x26, local copies, waits for them, and re-layouts  1.42 us
    pallas_call x1, Pallas kernels, early(): pl.pallas_call(early_kernel, out_shape=(points, points, jax.ShapeDtypeStr...  1.39 us
  transfers between devices with their start and end apart: 2, of which 2 were waited for; matrix products, arithmetic and copies ran while one was open for 0% of the time, Pallas kernels for 7%

profile of v4, /device:TPU:6, one launch (start us, length us, event | category | flops | bytes accessed | tf_op | source)
XLA Modules:
  0.0 50.3 jit_solution(5898872784485224003)
XLA Ops:
  0.0 0.7 %slice.3 = bf16[16,256]{1,0:T(8,128)(2,1)S(1)} slice(bf16[512,256]{1,0:T(8,128)(2,1)} %tokens_ref.1), slice={[496:512], [0:256]} | slice | bytes 16384 | tf_op jit(solution)/shard_map/slice | solution.py:332
  0.7 1.6 %collective-permute-start = (bf16[16,256]{1,0:T(8,128)(2,1)S(1)}, bf16[16,256]{1,0:T(8,128)(2,1)S(1)}, u32[]{:S(2)}, u32[]{:S(2)}) collective-permute-start(bf16[16,256]{1,0:T(8,128)(2,1)S(1)} %slice.3), channel_id=1, source_target_pairs={{0,1},{1,2},{2,3},{3,4},{4,5},{5,6},{6,7},{7,8},{8,9},{9,10},{10,1... | collective-permute-start | bytes 24584 | tf_op jit(solution)/shard_map/ppermute | solution.py:322
  2.3 0.1 add_convert_fusion
  2.4 1.8 %project.1 = (bf16[256,512]{1,0:T(8,128)(2,1)S(1)}, f32[8,512]{1,0:T(8,128)S(1)}, bf16[256,512]{1,0:T(8,128)(2,1)S(1)}, f32[3,768]{1,0:T(4,128)S(1)}) custom-call(bf16[512,256]{1,0:T(8,128)(2,1)} %tokens_ref.1, bf16[256,768]{1,0:T(8,128)(2,1)} %w_ref.2, f32[3,768]{1,0:T(4,128)} %taps_ref.1), custom_call_target="tpu_custom_call" | custom-call | flops 134217728 | bytes 2097152 | tf_op jit(solution)/shard_map/project/pallas_call | solution.py:82
  4.1 5.9 %collective-permute-done.rim_ref = bf16[16,256]{1,0:T(8,128)(2,1)S(1)} collective-permute-done((bf16[16,256]{1,0:T(8,128)(2,1)S(1)}, bf16[16,256]{1,0:T(8,128)(2,1)S(1)}, u32[]{:S(2)}, u32[]{:S(2)}) %collective-permute-start) | collective-permute-done | bytes 8224 | tf_op jit(solution)/shard_map/ppermute | solution.py:322
  10.0 0.1 broadcast_in_dim.2.there_ref
  10.1 0.3 fix_rim.1
  10.4 0.0 copy-start
  10.4 0.0 copy-start.6
  10.4 15.9 %all_to_all.10.own_ref = bf16[16,16,512]{2,1,0:T(8,128)(2,1)S(1)} all-to-all(bf16[16,16,512]{2,1,0:T(8,128)(2,1)S(1)} %bitcast.5), channel_id=1, replica_groups=mesh['span'=16,'tok'=16] {'tok'}, dimensions={0} | all-to-all | bytes 524288 | tf_op jit(solution)/shard_map/all_to_all | solution.py:335
  26.3 0.0 collective-permute-start.1
  26.3 0.7 %copy-done.12 = f32[16]{0:T(128)S(1)} copy-done((f32[16]{0:T(128)S(1)}, f32[16]{0:T(128)}, u32[]{:S(2)}) %copy-start.12) | copy-done | bytes 88
  27.0 0.1 copy.14.gain_ref
  27.1 0.0 copy-done.1
  27.1 0.0 copy-done.6
  27.1 0.0 copy-start.5
  27.1 0.0 copy-start.7
  27.1 0.0 copy-start.9
  27.1 0.0 copy-start.10
  27.1 0.0 copy-start.11
  27.1 0.4 make_query.1.query_ref
  27.5 0.4 copy-done.5
  27.9 0.2 copy-done.9
  28.1 0.1 copy-done.10
  28.2 1.4 %early.1 = (f32[1024,256]{1,0:T(8,128)S(1)}, f32[1024,256]{1,0:T(8,128)S(1)}, f32[16,16,512]{2,1,0:T(8,128)S(1)}) custom-call(bf16[16,8192]{1,0:T(8,128)(2,1)S(1)} %copy-done.9, bf16[16,16,512]{2,1,0:T(8,128)(2,1)S(1)} %all_to_all.10.own_ref, f32[16,1]{1,0:T(8,128)S(1)} %copy.14.gain_ref, bf16[128,128]{1,0:T(8,128)(2,1)S(1)} %copy-done.7, ...), custom_call_target="tpu_custom_call" | custom-call | flops 800000000 | bytes 3145728 | tf_op jit(solution)/shard_map/early/pallas_call | solution.py:219
  29.6 4.9 %collective-permute-done.1.past_ref = bf16[16,16,512]{2,1,0:T(8,128)(2,1)S(1)} collective-permute-done((bf16[16,16,512]{2,1,0:T(8,128)(2,1)S(1)}, bf16[16,16,512]{2,1,0:T(8,128)(2,1)S(1)}, u32[]{:S(2)}, u32[]{:S(2)}) %collective-permute-start.1) | collective-permute-done | bytes 262176 | tf_op jit(solution)/shard_map/ppermute | solution.py:322
  34.5 0.0 copy-done.3
  34.5 1.0 %convolve.1 = bf16[16,16,512]{2,1,0:T(8,128)(2,1)S(1)} custom-call(f32[2,256]{1,0:T(2,128)S(1)} %broadcast_in_dim.2.there_ref, bf16[16,16,512]{2,1,0:T(8,128)(2,1)S(1)} %collective-permute-done.1.past_ref, f32[1024,256]{1,0:T(8,128)S(1)} %get-tuple-element.18.spec_ref, f32[1024,256]{1,0:T(8,128)S(1)} %get-tuple-element.20.freq_ref, ...), custom_call_target="tpu_custom_call" | custom-call | flops 800000000 | bytes 4194304 | tf_op jit(solution)/shard_map/convolve/pallas_call | solution.py:274
  35.5 0.0 copy-start.2
  35.5 13.7 %all_to_all.11 = bf16[16,16,512]{2,1,0:T(8,128)(2,1)S(1)} all-to-all(bf16[16,16,512]{2,1,0:T(8,128)(2,1)S(1)} %convolve.1), channel_id=1, replica_groups=mesh['span'=16,'tok'=16] {'tok'}, dimensions={0} | all-to-all | bytes 524288 | tf_op jit(solution)/shard_map/all_to_all | solution.py:343
  49.3 0.0 copy-done.2
  49.3 1.0 %project_out.1 = bf16[512,256]{1,0:T(8,128)(2,1)} custom-call(bf16[256,512]{1,0:T(8,128)(2,1)S(1)} %bitcast.6, f32[512,256]{1,0:T(8,128)S(1)} %make_query.1.query_ref, bf16[256,256]{1,0:T(8,128)(2,1)S(1)} %copy-done.2), custom_call_target="tpu_custom_call" | custom-call | flops 67108864 | bytes 2097152 | tf_op jit(solution)/shard_map/project_out/pallas_call | solution.py:304
  (10 shorter events, 0.0 us)
Async XLA Ops:
  0.7 9.3 %collective-permute-start = (bf16[16,256]{1,0:T(8,128)(2,1)S(1)}, bf16[16,256]{1,0:T(8,128)(2,1)S(1)}, u32[]{:S(2)}, u32[]{:S(2)}) collective-permute-start(bf16[16,256]{1,0:T(8,128)(2,1)S(1)} %slice.3), channel_id=1, source_target_pairs={{0,1},{1,2},{2,3},{3,4},{4,5},{5,6},{6,7},{7,8},{8,9},{9,10},{10,1... | collective-permute-start | bytes 24584 | tf_op jit(solution)/shard_map/ppermute | solution.py:322
  10.1 17.0 %copy-start.1 = (bf16[512,256]{1,0:T(8,128)(2,1)S(1)}, bf16[512,256]{1,0:T(8,128)(2,1)}, u32[]{:S(2)}) copy-start(bf16[512,256]{1,0:T(8,128)(2,1)} %tokens_ref.1) | copy-start | bytes 786436
  10.4 16.7 %copy-start = (bf16[256,768]{1,0:T(8,128)(2,1)S(1)}, bf16[256,768]{1,0:T(8,128)(2,1)}, u32[]{:S(2)}) copy-start(bf16[256,768]{1,0:T(8,128)(2,1)} %w_ref.2) | copy-start | bytes 1179652
  10.4 16.7 %copy-start.6 = (f32[3,768]{1,0:T(4,128)S(1)}, f32[3,768]{1,0:T(4,128)}, u32[]{:S(2)}) copy-start(f32[3,768]{1,0:T(4,128)} %taps_ref.1) | copy-start | bytes 27652
  26.3 0.7 %copy-start.12 = (f32[16]{0:T(128)S(1)}, f32[16]{0:T(128)}, u32[]{:S(2)}) copy-start(f32[16]{0:T(128)} %param.17) | copy-start | bytes 196
  26.3 8.2 %collective-permute-start.1 = (bf16[16,16,512]{2,1,0:T(8,128)(2,1)S(1)}, bf16[16,16,512]{2,1,0:T(8,128)(2,1)S(1)}, u32[]{:S(2)}, u32[]{:S(2)}) collective-permute-start(bf16[16,16,512]{2,1,0:T(8,128)(2,1)S(1)} %all_to_all.10.own_ref), channel_id=1, source_target_pairs={{0,16},{16,32},{32,48},{48,64},{64,80},{80,96},{96,112},{112,128},... | collective-permute-start | bytes 786440 | tf_op jit(solution)/shard_map/ppermute | solution.py:322
  27.1 0.8 %copy-start.5 = (f32[2,64,128]{2,1,0:T(8,128)S(1)}, f32[2,64,128]{2,1,0:T(8,128)}, u32[]{:S(2)}) copy-start(f32[2,64,128]{2,1,0:T(8,128)} %constant.29.clone.twist_ref) | copy-start | bytes 196612
  27.1 0.8 %copy-start.7 = (bf16[128,128]{1,0:T(8,128)(2,1)S(1)}, bf16[128,128]{1,0:T(8,128)(2,1)}, u32[]{:S(2)}) copy-start(bf16[128,128]{1,0:T(8,128)(2,1)} %constant.23.clone.into_lo_ref) | copy-start | bytes 98308
  27.1 1.0 %copy-start.9 = (bf16[16,8192]{1,0:T(8,128)(2,1)S(1)}, bf16[16,8192]{1,0:T(8,128)(2,1)}, u32[]{:S(2)}) copy-start(bf16[16,8192]{1,0:T(8,128)(2,1)} %filter_ref.1) | copy-start | bytes 786436
  27.1 1.1 %copy-start.10 = (bf16[768,256]{1,0:T(8,128)(2,1)S(1)}, bf16[768,256]{1,0:T(8,128)(2,1)}, u32[]{:S(2)}) copy-start(bf16[768,256]{1,0:T(8,128)(2,1)} %constant.26.clone.cols_in_ref) | copy-start | bytes 1179652
  27.1 1.1 %copy-start.11 = (bf16[128,128]{1,0:T(8,128)(2,1)S(1)}, bf16[128,128]{1,0:T(8,128)(2,1)}, u32[]{:S(2)}) copy-start(bf16[128,128]{1,0:T(8,128)(2,1)} %constant.24.clone.into_hi_ref) | copy-start | bytes 98308
  28.2 6.3 %copy-start.3 = (bf16[256,256]{1,0:T(8,128)(2,1)S(1)}, bf16[256,256]{1,0:T(8,128)(2,1)}, u32[]{:S(2)}) copy-start(bf16[256,256]{1,0:T(8,128)(2,1)} %constant.25.clone.cols_in_ref) | copy-start | bytes 393220
  28.2 6.3 %copy-start.4 = (bf16[256,256]{1,0:T(8,128)(2,1)S(1)}, bf16[256,256]{1,0:T(8,128)(2,1)}, u32[]{:S(2)}) copy-start(bf16[256,256]{1,0:T(8,128)(2,1)} %constant.27.clone.cols_out_ref) | copy-start | bytes 393220
  28.2 6.3 %copy-start.8 = (bf16[64,256]{1,0:T(8,128)(2,1)S(1)}, bf16[64,256]{1,0:T(8,128)(2,1)}, u32[]{:S(2)}) copy-start(bf16[64,256]{1,0:T(8,128)(2,1)} %constant.28.clone.back_ref) | copy-start | bytes 98308
  35.5 13.8 %copy-start.2 = (bf16[256,256]{1,0:T(8,128)(2,1)S(1)}, bf16[256,256]{1,0:T(8,128)(2,1)}, u32[]{:S(2)}) copy-start(bf16[256,256]{1,0:T(8,128)(2,1)} %w_ref.3) | copy-start | bytes 393220

commit v5 on v4

--- a/solution.py
+++ b/solution.py
@@ -29,7 +29,7 @@
     twist = np.stack([twist.real, twist.imag]).astype(np.float32)
     high = bf(cols_in)
     wide = np.concatenate([high, bf(cols_in - high.astype(np.float64)), high], 0)
-    tables = pair(into[:, :HALF]), pair(into[:, HALF:]), high, wide, bf(cols_out), pair(back), twist
+    tables = pair(into[:, :HALF]), pair(into), high, wide, bf(cols_out), pair(back), twist
     return [jnp.asarray(table) for table in tables]
 
 
@@ -190,8 +190,8 @@
 
 
 def early_kernel(
-    filter_ref, own_ref, gain_ref, into_lo_ref, into_hi_ref, cols_in_ref, twist_ref, spec_ref,
-    freq_ref, skip_ref, rows_ref,
+    filter_ref, own_ref, gain_ref, into_lo_ref, cols_in_ref, twist_ref, spec_ref,
+    data_ref, skip_ref, rows_ref,
 ):
     chans, taps = filter_ref.shape
     tiles = taps // LANES
@@ -207,19 +207,21 @@
     data = by_channel(rows_ref, chans, 0, tiles).astype(jnp.bfloat16)
     spec_ref[...] = forward(into_lo_ref[...], cols_in_ref[...], *twist, data, chans)
     data = by_channel(rows_ref, chans, tiles, tiles)
-    freq_ref[...] = forward(
-        into_hi_ref[...], cols_in_ref[: 4 * LANES], *twist, data.astype(jnp.bfloat16), chans
-    )
-
-
-def early(long_filter, own, gain, into_lo, into_hi, cols_in, twist):
+    data_ref[...] = data.astype(jnp.bfloat16)
+
+
+def early(long_filter, own, gain, into_lo, cols_in, twist):
     chans, taps = long_filter.shape
     tiles = taps // LANES
     points = jax.ShapeDtypeStruct((chans * HALF, 2 * LANES), jnp.float32)
     return pl.pallas_call(
         early_kernel,
-        out_shape=(points, points, jax.ShapeDtypeStruct(own.shape, jnp.float32)),
-        in_specs=[VMEM] * 7,
+        out_shape=(
+            points,
+            jax.ShapeDtypeStruct((tiles, chans * LANES), jnp.bfloat16),
+            jax.ShapeDtypeStruct(own.shape, jnp.float32),
+        ),
+        in_specs=[VMEM] * 6,
         out_specs=(VMEM,) * 3,
         scratch_shapes=[pltpu.VMEM((2 * tiles * chans, LANES), jnp.float32)],
         compiler_params=pltpu.CompilerParams(vmem_limit_bytes=24 << 20),
@@ -227,11 +229,11 @@
             flops=800_000_000, bytes_accessed=3 << 20, transcendentals=0
         ),
         name="early",
-    )(long_filter, own, gain, into_lo, into_hi, cols_in, twist)
+    )(long_filter, own, gain, into_lo, cols_in, twist)
 
 
 def convolve_kernel(
-    there_ref, past_ref, spec_ref, freq_ref, skip_ref, into_lo_ref, cols_in_ref, cols_out_ref,
+    there_ref, past_ref, spec_ref, data_ref, skip_ref, into_ref, cols_in_ref, cols_out_ref,
     back_ref, twist_ref, out_ref, rows_ref,
 ):
     peers, chans, width = out_ref.shape
@@ -243,7 +245,8 @@
     load = rows_of(past_ref)
     put_rows(lambda i: jnp.where(there, load(i).astype(jnp.float32), 0.0), rows_ref, chans, tiles, 0)
     past = by_channel(rows_ref, chans, 0, tiles).astype(jnp.bfloat16)
-    freq = forward(into_lo_ref[...], cols_in_ref[...], twist_re, twist_im, past, chans) + freq_ref[...]
+    data = jnp.concatenate([past, data_ref[...]], axis=0)
+    freq = forward(into_ref[...], cols_in_ref[...], twist_re, twist_im, data, chans)
     spec = spec_ref[...]
     fre, fim = freq[:, :LANES], freq[:, LANES:]
     sre, sim = spec[:, :LANES], spec[:, LANES:]
@@ -269,7 +272,7 @@
         out_ref[tile // per, :, lanes] = out.astype(jnp.bfloat16)
 
 
-def convolve(there, past, spec, freq, skip, into_lo, cols_in, cols_out, back, twist):
+def convolve(there, past, spec, data, skip, into, cols_in, cols_out, back, twist):
     peers, chans, width = past.shape
     return pl.pallas_call(
         convolve_kernel,
@@ -282,7 +285,7 @@
             flops=800_000_000, bytes_accessed=4 << 20, transcendentals=0
         ),
         name="convolve",
-    )(there, past, spec, freq, skip, into_lo, cols_in, cols_out, back, twist)
+    )(there, past, spec, data, skip, into, cols_in, cols_out, back, twist)
 
 
 def output_kernel(conv_ref, query_ref, w_ref, out_hbm, out_ref, sems):
@@ -325,7 +328,7 @@
 def per_device(tokens, w_in, short_filter, long_filter, skip_gain, w_out):
     rows = tokens.shape[0]
     peers = lax.axis_size("tok")
-    into_lo, into_hi, cols_in, cols_wide, cols_out, back, twist = dft_tables()
+    into_lo, into, cols_in, cols_wide, cols_out, back, twist = dft_tables()
     span = lax.axis_index("span")
     there = jnp.stack([span + lax.axis_index("tok") > 0, span > 0]).astype(jnp.float32)
     there = jnp.broadcast_to(there[:, None], (2, D))
@@ -336,10 +339,12 @@
         product.reshape(peers, D // peers, rows), "tok", split_axis=0, concat_axis=0, tiled=True
     )
     past = rotated(own, "span")
-    spec, freq, skip = early(long_filter, own, skip_gain.reshape(-1, 1), into_lo, into_hi, cols_wide, twist)
+    spec, data, skip = early(
+        long_filter, own, skip_gain.reshape(-1, 1), into_lo, cols_wide, twist
+    )
     query = make_query(there, tokens, rim, w_in, short_filter)
-    freq, query = lax.optimization_barrier((freq, query))
-    conv = convolve(there, past, spec, freq, skip, into_lo, cols_in, cols_out, back, twist)
+    data, query = lax.optimization_barrier((data, query))
+    conv = convolve(there, past, spec, data, skip, into, cols_in, cols_out, back, twist)
     conv = lax.all_to_all(conv, "tok", split_axis=0, concat_axis=0, tiled=True)
     return project_out(conv.reshape(D, rows), query, w_out)
 

time: 50.5 us -> 50.6 us (level)
  transfers between devices with their start and end apart: 2 -> 2, of which waited for: 2 -> 2; matrix products, arithmetic and copies ran while one was open for 0% -> 0% of each run, Pallas kernels for 7% -> 6%
where the time goes in v5:
time: 50.6 us; the launch traced here: 50.3 us
  blocking collectives  29.7 us (59%)
  waiting for transfers between devices  11.3 us (22%)
  Pallas kernels  5.34 us (11%)
  local copies, waits for them, and re-layouts  2.24 us (4%)
  starting transfers between devices  1.58 us (3%)
    all_to_all x1, blocking collectives, per_device(): lax.all_to_all(product.reshape(peers, D // peers, rows), 'tok', split_axi...  15.9 us
    all_to_all x1, blocking collectives, per_device(): conv = lax.all_to_all(conv, 'tok', split_axis=0, concat_axis=0, tiled=True)  13.7 us
    ppermute x2, waiting for transfers between devices, rotated(): lax.ppermute(array, axes, [(i, (i + 1) % count) for i in range(count)])  11.3 us
    pallas_call x1, Pallas kernels, project(): pl.pallas_call(project_kernel, out_shape=(jax.ShapeDtypeStruct((D, rows),...  1.75 us
    ppermute x2, starting transfers between devices, rotated(): lax.ppermute(array, axes, [(i, (i + 1) % count) for i in range(count)])  1.58 us
    unnamed x26, local copies, waits for them, and re-layouts  1.39 us
  transfers between devices with their start and end apart: 2, of which 2 were waited for; matrix products, arithmetic and copies ran while one was open for 0% of the time, Pallas kernels for 6%

profile of v5, /device:TPU:6, one launch (start us, length us, event | category | flops | bytes accessed | tf_op | source)
XLA Modules:
  0.0 50.3 jit_solution(13432539410608864882)
XLA Ops:
  0.0 0.7 %slice.3 = bf16[16,256]{1,0:T(8,128)(2,1)S(1)} slice(bf16[512,256]{1,0:T(8,128)(2,1)} %tokens_ref.1), slice={[496:512], [0:256]} | slice | bytes 16384 | tf_op jit(solution)/shard_map/slice | solution.py:335
  0.7 1.6 %collective-permute-start = (bf16[16,256]{1,0:T(8,128)(2,1)S(1)}, bf16[16,256]{1,0:T(8,128)(2,1)S(1)}, u32[]{:S(2)}, u32[]{:S(2)}) collective-permute-start(bf16[16,256]{1,0:T(8,128)(2,1)S(1)} %slice.3), channel_id=1, source_target_pairs={{0,1},{1,2},{2,3},{3,4},{4,5},{5,6},{6,7},{7,8},{8,9},{9,10},{10,1... | collective-permute-start | bytes 24584 | tf_op jit(solution)/shard_map/ppermute | solution.py:325
  2.3 0.1 add_convert_fusion
  2.4 1.8 %project.1 = (bf16[256,512]{1,0:T(8,128)(2,1)S(1)}, f32[8,512]{1,0:T(8,128)S(1)}, bf16[256,512]{1,0:T(8,128)(2,1)S(1)}, f32[3,768]{1,0:T(4,128)S(1)}) custom-call(bf16[512,256]{1,0:T(8,128)(2,1)} %tokens_ref.1, bf16[256,768]{1,0:T(8,128)(2,1)} %w_ref.2, f32[3,768]{1,0:T(4,128)} %taps_ref.1), custom_call_target="tpu_custom_call" | custom-call | flops 134217728 | bytes 2097152 | tf_op jit(solution)/shard_map/project/pallas_call | solution.py:82
  4.1 5.9 %collective-permute-done.rim_ref = bf16[16,256]{1,0:T(8,128)(2,1)S(1)} collective-permute-done((bf16[16,256]{1,0:T(8,128)(2,1)S(1)}, bf16[16,256]{1,0:T(8,128)(2,1)S(1)}, u32[]{:S(2)}, u32[]{:S(2)}) %collective-permute-start) | collective-permute-done | bytes 8224 | tf_op jit(solution)/shard_map/ppermute | solution.py:325
  10.0 0.1 broadcast_in_dim.2.there_ref
  10.1 0.3 fix_rim.1
  10.4 0.0 copy-start
  10.4 0.0 copy-start.3
  10.4 15.9 %all_to_all.10.own_ref = bf16[16,16,512]{2,1,0:T(8,128)(2,1)S(1)} all-to-all(bf16[16,16,512]{2,1,0:T(8,128)(2,1)S(1)} %bitcast.5), channel_id=1, replica_groups=mesh['span'=16,'tok'=16] {'tok'}, dimensions={0} | all-to-all | bytes 524288 | tf_op jit(solution)/shard_map/all_to_all | solution.py:338
  26.3 0.0 collective-permute-start.1
  26.3 0.7 %copy-done.12 = f32[16]{0:T(128)S(1)} copy-done((f32[16]{0:T(128)S(1)}, f32[16]{0:T(128)}, u32[]{:S(2)}) %copy-start.12) | copy-done | bytes 88
  27.0 0.1 copy.14.gain_ref
  27.1 0.0 copy-done.1
  27.1 0.0 copy-done
  27.1 0.0 copy-done.3
  27.1 0.0 copy-start.4
  27.1 0.0 copy-start.5
  27.1 0.0 copy-start.8
  27.1 0.0 copy-start.11
  27.1 0.4 make_query.1.query_ref
  27.5 0.5 %copy-done.4 = bf16[16,8192]{1,0:T(8,128)(2,1)S(1)} copy-done((bf16[16,8192]{1,0:T(8,128)(2,1)S(1)}, bf16[16,8192]{1,0:T(8,128)(2,1)}, u32[]{:S(2)}) %copy-start.4) | copy-done | bytes 262168
  28.0 0.1 copy-done.5
  28.2 0.0 copy-start.9
  28.2 0.0 copy-start.10
  28.2 1.0 %early.1 = (f32[1024,256]{1,0:T(8,128)S(1)}, bf16[64,2048]{1,0:T(8,128)(2,1)S(1)}, f32[16,16,512]{2,1,0:T(8,128)S(1)}) custom-call(bf16[16,8192]{1,0:T(8,128)(2,1)S(1)} %copy-done.4, bf16[16,16,512]{2,1,0:T(8,128)(2,1)S(1)} %all_to_all.10.own_ref, f32[16,1]{1,0:T(8,128)S(1)} %copy.14.gain_ref, bf16[128,128]{1,0:T(8,128)(2,1)S(1)} %copy-done.11, ...), custom_call_target="tpu_custom_call" | custom-call | flops 800000000 | bytes 3145728 | tf_op jit(solution)/shard_map/early/pallas_call | solution.py:217
  29.2 5.4 %collective-permute-done.1.past_ref = bf16[16,16,512]{2,1,0:T(8,128)(2,1)S(1)} collective-permute-done((bf16[16,16,512]{2,1,0:T(8,128)(2,1)S(1)}, bf16[16,16,512]{2,1,0:T(8,128)(2,1)S(1)}, u32[]{:S(2)}, u32[]{:S(2)}) %collective-permute-start.1) | collective-permute-done | bytes 262176 | tf_op jit(solution)/shard_map/ppermute | solution.py:325
  34.5 0.0 copy-done.6
  34.5 1.0 %convolve.1 = bf16[16,16,512]{2,1,0:T(8,128)(2,1)S(1)} custom-call(f32[2,256]{1,0:T(2,128)S(1)} %broadcast_in_dim.2.there_ref, bf16[16,16,512]{2,1,0:T(8,128)(2,1)S(1)} %collective-permute-done.1.past_ref, f32[1024,256]{1,0:T(8,128)S(1)} %get-tuple-element.18.spec_ref, bf16[64,2048]{1,0:T(8,128)(2,1)S(1)} %get-tuple-element.20.data_ref, ...), custom_call_target="tpu_custom_call" | custom-call | flops 800000000 | bytes 4194304 | tf_op jit(solution)/shard_map/convolve/pallas_call | solution.py:277
  35.6 0.0 copy-start.2
  35.6 13.7 %all_to_all.11 = bf16[16,16,512]{2,1,0:T(8,128)(2,1)S(1)} all-to-all(bf16[16,16,512]{2,1,0:T(8,128)(2,1)S(1)} %convolve.1), channel_id=1, replica_groups=mesh['span'=16,'tok'=16] {'tok'}, dimensions={0} | all-to-all | bytes 524288 | tf_op jit(solution)/shard_map/all_to_all | solution.py:348
  49.3 1.0 %project_out.1 = bf16[512,256]{1,0:T(8,128)(2,1)} custom-call(bf16[256,512]{1,0:T(8,128)(2,1)S(1)} %bitcast.6, f32[512,256]{1,0:T(8,128)S(1)} %make_query.1.query_ref, bf16[256,256]{1,0:T(8,128)(2,1)S(1)} %copy-done.2), custom_call_target="tpu_custom_call" | custom-call | flops 67108864 | bytes 2097152 | tf_op jit(solution)/shard_map/project_out/pallas_call | solution.py:307
  (10 shorter events, 0.0 us)
Async XLA Ops:
  0.7 9.3 %collective-permute-start = (bf16[16,256]{1,0:T(8,128)(2,1)S(1)}, bf16[16,256]{1,0:T(8,128)(2,1)S(1)}, u32[]{:S(2)}, u32[]{:S(2)}) collective-permute-start(bf16[16,256]{1,0:T(8,128)(2,1)S(1)} %slice.3), channel_id=1, source_target_pairs={{0,1},{1,2},{2,3},{3,4},{4,5},{5,6},{6,7},{7,8},{8,9},{9,10},{10,1... | collective-permute-start | bytes 24584 | tf_op jit(solution)/shard_map/ppermute | solution.py:325
  10.1 17.0 %copy-start.1 = (bf16[512,256]{1,0:T(8,128)(2,1)S(1)}, bf16[512,256]{1,0:T(8,128)(2,1)}, u32[]{:S(2)}) copy-start(bf16[512,256]{1,0:T(8,128)(2,1)} %tokens_ref.1) | copy-start | bytes 786436
  10.4 16.7 %copy-start = (bf16[256,768]{1,0:T(8,128)(2,1)S(1)}, bf16[256,768]{1,0:T(8,128)(2,1)}, u32[]{:S(2)}) copy-start(bf16[256,768]{1,0:T(8,128)(2,1)} %w_ref.2) | copy-start | bytes 1179652
  10.4 16.7 %copy-start.3 = (f32[3,768]{1,0:T(4,128)S(1)}, f32[3,768]{1,0:T(4,128)}, u32[]{:S(2)}) copy-start(f32[3,768]{1,0:T(4,128)} %taps_ref.1) | copy-start | bytes 27652
  26.3 0.7 %copy-start.12 = (f32[16]{0:T(128)S(1)}, f32[16]{0:T(128)}, u32[]{:S(2)}) copy-start(f32[16]{0:T(128)} %param.17) | copy-start | bytes 196
  26.3 8.2 %collective-permute-start.1 = (bf16[16,16,512]{2,1,0:T(8,128)(2,1)S(1)}, bf16[16,16,512]{2,1,0:T(8,128)(2,1)S(1)}, u32[]{:S(2)}, u32[]{:S(2)}) collective-permute-start(bf16[16,16,512]{2,1,0:T(8,128)(2,1)S(1)} %all_to_all.10.own_ref), channel_id=1, source_target_pairs={{0,16},{16,32},{32,48},{48,64},{64,80},{80,96},{96,112},{112,128},... | collective-permute-start | bytes 786440 | tf_op jit(solution)/shard_map/ppermute | solution.py:325
  27.1 1.0 %copy-start.4 = (bf16[16,8192]{1,0:T(8,128)(2,1)S(1)}, bf16[16,8192]{1,0:T(8,128)(2,1)}, u32[]{:S(2)}) copy-start(bf16[16,8192]{1,0:T(8,128)(2,1)} %filter_ref.1) | copy-start | bytes 786436
  27.1 1.1 %copy-start.5 = (bf16[768,256]{1,0:T(8,128)(2,1)S(1)}, bf16[768,256]{1,0:T(8,128)(2,1)}, u32[]{:S(2)}) copy-start(bf16[768,256]{1,0:T(8,128)(2,1)} %constant.26.clone.cols_in_ref) | copy-start | bytes 1179652
  27.1 1.1 %copy-start.8 = (f32[2,64,128]{2,1,0:T(8,128)S(1)}, f32[2,64,128]{2,1,0:T(8,128)}, u32[]{:S(2)}) copy-start(f32[2,64,128]{2,1,0:T(8,128)} %constant.29.clone.twist_ref) | copy-start | bytes 196612
  27.1 1.1 %copy-start.11 = (bf16[128,128]{1,0:T(8,128)(2,1)S(1)}, bf16[128,128]{1,0:T(8,128)(2,1)}, u32[]{:S(2)}) copy-start(bf16[128,128]{1,0:T(8,128)(2,1)} %constant.23.clone.into_lo_ref) | copy-start | bytes 98308
  28.2 6.4 %copy-start.6 = (bf16[256,256]{1,0:T(8,128)(2,1)S(1)}, bf16[256,256]{1,0:T(8,128)(2,1)}, u32[]{:S(2)}) copy-start(bf16[256,256]{1,0:T(8,128)(2,1)} %constant.25.clone.cols_in_ref) | copy-start | bytes 393220
  28.2 6.4 %copy-start.7 = (bf16[256,256]{1,0:T(8,128)(2,1)S(1)}, bf16[256,256]{1,0:T(8,128)(2,1)}, u32[]{:S(2)}) copy-start(bf16[256,256]{1,0:T(8,128)(2,1)} %constant.27.clone.cols_out_ref) | copy-start | bytes 393220
  28.2 6.4 %copy-start.9 = (bf16[128,256]{1,0:T(8,128)(2,1)S(1)}, bf16[128,256]{1,0:T(8,128)(2,1)}, u32[]{:S(2)}) copy-start(bf16[128,256]{1,0:T(8,128)(2,1)} %constant.24.clone.into_ref) | copy-start | bytes 196612
  28.2 6.4 %copy-start.10 = (bf16[64,256]{1,0:T(8,128)(2,1)S(1)}, bf16[64,256]{1,0:T(8,128)(2,1)}, u32[]{:S(2)}) copy-start(bf16[64,256]{1,0:T(8,128)(2,1)} %constant.28.clone.back_ref) | copy-start | bytes 98308
  35.6 13.8 %copy-start.2 = (bf16[256,256]{1,0:T(8,128)(2,1)S(1)}, bf16[256,256]{1,0:T(8,128)(2,1)}, u32[]{:S(2)}) copy-start(bf16[256,256]{1,0:T(8,128)(2,1)} %w_ref.3) | copy-start | bytes 393220

commit v6 on v4

--- a/solution.py
+++ b/solution.py
@@ -329,8 +329,10 @@
     span = lax.axis_index("span")
     there = jnp.stack([span + lax.axis_index("tok") > 0, span > 0]).astype(jnp.float32)
     there = jnp.broadcast_to(there[:, None], (2, D))
+    w_in, there = lax.optimization_barrier((w_in, there))
     rim = rotated(tokens[rows - RIM :], ("span", "tok"))
     product, head, w_part, taps = project(tokens, w_in, short_filter)
+    head, there, rim = lax.optimization_barrier((head, there, rim))
     product = fix_rim(there, rim, w_part, taps, head, product)
     own = lax.all_to_all(
         product.reshape(peers, D // peers, rows), "tok", split_axis=0, concat_axis=0, tiled=True

time: 50.5 us -> 50.5 us (level)
  no operation moved by 1% of the time
where the time goes in v6:
time: 50.5 us; the launch traced here: 50.2 us
  blocking collectives  29.7 us (59%)
  waiting for transfers between devices  10.8 us (21%)
  Pallas kernels  5.75 us (11%)
  local copies, waits for them, and re-layouts  2.27 us (4%)
  starting transfers between devices  1.58 us (3%)
    all_to_all x1, blocking collectives, per_device(): lax.all_to_all(product.reshape(peers, D // peers, rows), 'tok', split_axi...  15.9 us
    all_to_all x1, blocking collectives, per_device(): conv = lax.all_to_all(conv, 'tok', split_axis=0, concat_axis=0, tiled=True)  13.7 us
    ppermute x2, waiting for transfers between devices, rotated(): lax.ppermute(array, axes, [(i, (i + 1) % count) for i in range(count)])  10.8 us
    pallas_call x1, Pallas kernels, project(): pl.pallas_call(project_kernel, out_shape=(jax.ShapeDtypeStruct((D, rows),...  1.75 us
    ppermute x2, starting transfers between devices, rotated(): lax.ppermute(array, axes, [(i, (i + 1) % count) for i in range(count)])  1.58 us
    unnamed x26, local copies, waits for them, and re-layouts  1.42 us
    pallas_call x1, Pallas kernels, early(): pl.pallas_call(early_kernel, out_shape=(points, points, jax.ShapeDtypeStr...  1.38 us
  transfers between devices with their start and end apart: 2, of which 2 were waited for; matrix products, arithmetic and copies ran while one was open for 0% of the time, Pallas kernels for 7%

profile of v6, /device:TPU:6, one launch (start us, length us, event | category | flops | bytes accessed | tf_op | source)
XLA Modules:
  0.0 50.2 jit_solution(12018336890583569152)
XLA Ops:
  0.0 0.7 %slice.3 = bf16[16,256]{1,0:T(8,128)(2,1)S(1)} slice(bf16[512,256]{1,0:T(8,128)(2,1)} %tokens_ref.1), slice={[496:512], [0:256]} | slice | bytes 16384 | tf_op jit(solution)/shard_map/slice | solution.py:333
  0.7 1.6 %collective-permute-start = (bf16[16,256]{1,0:T(8,128)(2,1)S(1)}, bf16[16,256]{1,0:T(8,128)(2,1)S(1)}, u32[]{:S(2)}, u32[]{:S(2)}) collective-permute-start(bf16[16,256]{1,0:T(8,128)(2,1)S(1)} %slice.3), channel_id=1, source_target_pairs={{0,1},{1,2},{2,3},{3,4},{4,5},{5,6},{6,7},{7,8},{8,9},{9,10},{10,1... | collective-permute-start | bytes 24584 | tf_op jit(solution)/shard_map/ppermute | solution.py:322
  2.3 0.1 add_convert_fusion
  2.4 0.1 broadcast_in_dim.2.there_ref
  2.4 1.8 %project.1 = (bf16[256,512]{1,0:T(8,128)(2,1)S(1)}, f32[8,512]{1,0:T(8,128)S(1)}, bf16[256,512]{1,0:T(8,128)(2,1)S(1)}, f32[3,768]{1,0:T(4,128)S(1)}) custom-call(bf16[512,256]{1,0:T(8,128)(2,1)} %tokens_ref.1, bf16[256,768]{1,0:T(8,128)(2,1)} %w_ref.1, f32[3,768]{1,0:T(4,128)} %taps_ref.1), custom_call_target="tpu_custom_call" | custom-call | flops 134217728 | bytes 2097152 | tf_op jit(solution)/shard_map/project/pallas_call | solution.py:82
  4.2 5.9 %collective-permute-done.rim_ref = bf16[16,256]{1,0:T(8,128)(2,1)S(1)} collective-permute-done((bf16[16,256]{1,0:T(8,128)(2,1)S(1)}, bf16[16,256]{1,0:T(8,128)(2,1)S(1)}, u32[]{:S(2)}, u32[]{:S(2)}) %collective-permute-start) | collective-permute-done | bytes 8224 | tf_op jit(solution)/shard_map/ppermute | solution.py:322
  10.0 0.3 fix_rim.1
  10.3 0.0 copy-start
  10.3 0.0 copy-start.6
  10.3 15.9 %all_to_all.10.own_ref = bf16[16,16,512]{2,1,0:T(8,128)(2,1)S(1)} all-to-all(bf16[16,16,512]{2,1,0:T(8,128)(2,1)S(1)} %bitcast.5), channel_id=1, replica_groups=mesh['span'=16,'tok'=16] {'tok'}, dimensions={0} | all-to-all | bytes 524288 | tf_op jit(solution)/shard_map/all_to_all | solution.py:337
  26.3 0.0 collective-permute-start.1
  26.3 0.7 %copy-done.12 = f32[16]{0:T(128)S(1)} copy-done((f32[16]{0:T(128)S(1)}, f32[16]{0:T(128)}, u32[]{:S(2)}) %copy-start.12) | copy-done | bytes 88
  26.9 0.1 copy.14.gain_ref
  27.0 0.0 copy-start.5
  27.0 0.0 copy-start.7
  27.0 0.0 copy-start.9
  27.0 0.0 copy-start.10
  27.1 0.0 copy-start.11
  27.1 0.4 make_query.1.query_ref
  27.4 0.4 copy-done.5
  27.8 0.0 copy-done.7
  27.9 0.2 copy-done.9
  28.0 0.1 copy-done.10
  28.1 0.0 copy-done.11
  28.2 1.4 %early.1 = (f32[1024,256]{1,0:T(8,128)S(1)}, f32[1024,256]{1,0:T(8,128)S(1)}, f32[16,16,512]{2,1,0:T(8,128)S(1)}) custom-call(bf16[16,8192]{1,0:T(8,128)(2,1)S(1)} %copy-done.9, bf16[16,16,512]{2,1,0:T(8,128)(2,1)S(1)} %all_to_all.10.own_ref, f32[16,1]{1,0:T(8,128)S(1)} %copy.14.gain_ref, bf16[128,128]{1,0:T(8,128)(2,1)S(1)} %copy-done.7, ...), custom_call_target="tpu_custom_call" | custom-call | flops 800000000 | bytes 3145728 | tf_op jit(solution)/shard_map/early/pallas_call | solution.py:219
  29.5 4.9 %collective-permute-done.1.past_ref = bf16[16,16,512]{2,1,0:T(8,128)(2,1)S(1)} collective-permute-done((bf16[16,16,512]{2,1,0:T(8,128)(2,1)S(1)}, bf16[16,16,512]{2,1,0:T(8,128)(2,1)S(1)}, u32[]{:S(2)}, u32[]{:S(2)}) %collective-permute-start.1) | collective-permute-done | bytes 262176 | tf_op jit(solution)/shard_map/ppermute | solution.py:322
  34.5 0.0 copy-done.4
  34.5 1.0 %convolve.1 = bf16[16,16,512]{2,1,0:T(8,128)(2,1)S(1)} custom-call(f32[2,256]{1,0:T(2,128)S(1)} %broadcast_in_dim.2.there_ref, bf16[16,16,512]{2,1,0:T(8,128)(2,1)S(1)} %collective-permute-done.1.past_ref, f32[1024,256]{1,0:T(8,128)S(1)} %get-tuple-element.28.spec_ref, f32[1024,256]{1,0:T(8,128)S(1)} %get-tuple-element.30.freq_ref, ...), custom_call_target="tpu_custom_call" | custom-call | flops 800000000 | bytes 4194304 | tf_op jit(solution)/shard_map/convolve/pallas_call | solution.py:274
  35.5 0.0 copy-start.2
  35.5 13.7 %all_to_all.11 = bf16[16,16,512]{2,1,0:T(8,128)(2,1)S(1)} all-to-all(bf16[16,16,512]{2,1,0:T(8,128)(2,1)S(1)} %convolve.1), channel_id=1, replica_groups=mesh['span'=16,'tok'=16] {'tok'}, dimensions={0} | all-to-all | bytes 524288 | tf_op jit(solution)/shard_map/all_to_all | solution.py:345
  49.2 0.0 copy-done.2
  49.2 1.0 %project_out.1 = bf16[512,256]{1,0:T(8,128)(2,1)} custom-call(bf16[256,512]{1,0:T(8,128)(2,1)S(1)} %bitcast.6, f32[512,256]{1,0:T(8,128)S(1)} %make_query.1.query_ref, bf16[256,256]{1,0:T(8,128)(2,1)S(1)} %copy-done.2), custom_call_target="tpu_custom_call" | custom-call | flops 67108864 | bytes 2097152 | tf_op jit(solution)/shard_map/project_out/pallas_call | solution.py:304
  (10 shorter events, 0.0 us)
Async XLA Ops:
  0.7 9.3 %collective-permute-start = (bf16[16,256]{1,0:T(8,128)(2,1)S(1)}, bf16[16,256]{1,0:T(8,128)(2,1)S(1)}, u32[]{:S(2)}, u32[]{:S(2)}) collective-permute-start(bf16[16,256]{1,0:T(8,128)(2,1)S(1)} %slice.3), channel_id=1, source_target_pairs={{0,1},{1,2},{2,3},{3,4},{4,5},{5,6},{6,7},{7,8},{8,9},{9,10},{10,1... | collective-permute-start | bytes 24584 | tf_op jit(solution)/shard_map/ppermute | solution.py:322
  10.0 17.0 %copy-start.1 = (bf16[512,256]{1,0:T(8,128)(2,1)S(1)}, bf16[512,256]{1,0:T(8,128)(2,1)}, u32[]{:S(2)}) copy-start(bf16[512,256]{1,0:T(8,128)(2,1)} %tokens_ref.1) | copy-start | bytes 786436
  10.3 16.7 %copy-start = (bf16[256,768]{1,0:T(8,128)(2,1)S(1)}, bf16[256,768]{1,0:T(8,128)(2,1)}, u32[]{:S(2)}) copy-start(bf16[256,768]{1,0:T(8,128)(2,1)} %w_ref.1) | copy-start | bytes 1179652
  10.3 16.7 %copy-start.6 = (f32[3,768]{1,0:T(4,128)S(1)}, f32[3,768]{1,0:T(4,128)}, u32[]{:S(2)}) copy-start(f32[3,768]{1,0:T(4,128)} %taps_ref.1) | copy-start | bytes 27652
  26.3 0.7 %copy-start.12 = (f32[16]{0:T(128)S(1)}, f32[16]{0:T(128)}, u32[]{:S(2)}) copy-start(f32[16]{0:T(128)} %param.17) | copy-start | bytes 196
  26.3 8.2 %collective-permute-start.1 = (bf16[16,16,512]{2,1,0:T(8,128)(2,1)S(1)}, bf16[16,16,512]{2,1,0:T(8,128)(2,1)S(1)}, u32[]{:S(2)}, u32[]{:S(2)}) collective-permute-start(bf16[16,16,512]{2,1,0:T(8,128)(2,1)S(1)} %all_to_all.10.own_ref), channel_id=1, source_target_pairs={{0,16},{16,32},{32,48},{48,64},{64,80},{80,96},{96,112},{112,128},... | collective-permute-start | bytes 786440 | tf_op jit(solution)/shard_map/ppermute | solution.py:322
  27.0 0.8 %copy-start.5 = (f32[2,64,128]{2,1,0:T(8,128)S(1)}, f32[2,64,128]{2,1,0:T(8,128)}, u32[]{:S(2)}) copy-start(f32[2,64,128]{2,1,0:T(8,128)} %constant.29.clone.twist_ref) | copy-start | bytes 196612
  27.0 0.8 %copy-start.7 = (bf16[128,128]{1,0:T(8,128)(2,1)S(1)}, bf16[128,128]{1,0:T(8,128)(2,1)}, u32[]{:S(2)}) copy-start(bf16[128,128]{1,0:T(8,128)(2,1)} %constant.23.clone.into_lo_ref) | copy-start | bytes 98308
  27.0 1.0 %copy-start.9 = (bf16[16,8192]{1,0:T(8,128)(2,1)S(1)}, bf16[16,8192]{1,0:T(8,128)(2,1)}, u32[]{:S(2)}) copy-start(bf16[16,8192]{1,0:T(8,128)(2,1)} %filter_ref.1) | copy-start | bytes 786436
  27.0 1.1 %copy-start.10 = (bf16[768,256]{1,0:T(8,128)(2,1)S(1)}, bf16[768,256]{1,0:T(8,128)(2,1)}, u32[]{:S(2)}) copy-start(bf16[768,256]{1,0:T(8,128)(2,1)} %constant.26.clone.cols_in_ref) | copy-start | bytes 1179652
  27.1 1.1 %copy-start.11 = (bf16[128,128]{1,0:T(8,128)(2,1)S(1)}, bf16[128,128]{1,0:T(8,128)(2,1)}, u32[]{:S(2)}) copy-start(bf16[128,128]{1,0:T(8,128)(2,1)} %constant.24.clone.into_hi_ref) | copy-start | bytes 98308
  28.1 6.3 %copy-start.3 = (bf16[256,256]{1,0:T(8,128)(2,1)S(1)}, bf16[256,256]{1,0:T(8,128)(2,1)}, u32[]{:S(2)}) copy-start(bf16[256,256]{1,0:T(8,128)(2,1)} %constant.25.clone.cols_in_ref) | copy-start | bytes 393220
  28.1 6.3 %copy-start.4 = (bf16[256,256]{1,0:T(8,128)(2,1)S(1)}, bf16[256,256]{1,0:T(8,128)(2,1)}, u32[]{:S(2)}) copy-start(bf16[256,256]{1,0:T(8,128)(2,1)} %constant.27.clone.cols_out_ref) | copy-start | bytes 393220
  28.1 6.3 %copy-start.8 = (bf16[64,256]{1,0:T(8,128)(2,1)S(1)}, bf16[64,256]{1,0:T(8,128)(2,1)}, u32[]{:S(2)}) copy-start(bf16[64,256]{1,0:T(8,128)(2,1)} %constant.28.clone.back_ref) | copy-start | bytes 98308
  35.5 13.8 %copy-start.2 = (bf16[256,256]{1,0:T(8,128)(2,1)S(1)}, bf16[256,256]{1,0:T(8,128)(2,1)}, u32[]{:S(2)}) copy-start(bf16[256,256]{1,0:T(8,128)(2,1)} %w_ref.2) | copy-start | bytes 393220

commit v7 on v6

--- a/solution.py
+++ b/solution.py
@@ -40,7 +40,7 @@
 VMEM = pl.BlockSpec(memory_space=pltpu.VMEM)
 HBM = pl.BlockSpec(memory_space=pltpu.MemorySpace.HBM)
 HEAD = 8
-PIECES = 2
+PIECES = 4
 
 
 def short_filter_sum(taps, now, one, two):

time: 50.5 us -> 50.5 us (level)
  no operation moved by 1% of the time
where the time goes in v7:
time: 50.5 us; the launch traced here: 50.2 us
  blocking collectives  29.7 us (59%)
  waiting for transfers between devices  10.8 us (21%)
  Pallas kernels  5.72 us (11%)
  local copies, waits for them, and re-layouts  2.27 us (4%)
  starting transfers between devices  1.58 us (3%)
    all_to_all x1, blocking collectives, per_device(): lax.all_to_all(product.reshape(peers, D // peers, rows), 'tok', split_axi...  15.9 us
    all_to_all x1, blocking collectives, per_device(): conv = lax.all_to_all(conv, 'tok', split_axis=0, concat_axis=0, tiled=True)  13.7 us
    ppermute x2, waiting for transfers between devices, rotated(): lax.ppermute(array, axes, [(i, (i + 1) % count) for i in range(count)])  10.8 us
    pallas_call x1, Pallas kernels, project(): pl.pallas_call(project_kernel, out_shape=(jax.ShapeDtypeStruct((D, rows),...  1.75 us
    ppermute x2, starting transfers between devices, rotated(): lax.ppermute(array, axes, [(i, (i + 1) % count) for i in range(count)])  1.58 us
    unnamed x26, local copies, waits for them, and re-layouts  1.42 us
    pallas_call x1, Pallas kernels, early(): pl.pallas_call(early_kernel, out_shape=(points, points, jax.ShapeDtypeStr...  1.38 us
  transfers between devices with their start and end apart: 2, of which 2 were waited for; matrix products, arithmetic and copies ran while one was open for 0% of the time, Pallas kernels for 7%

profile of v7, /device:TPU:6, one launch (start us, length us, event | category | flops | bytes accessed | tf_op | source)
XLA Modules:
  0.0 50.2 jit_solution(2133972418110456387)
XLA Ops:
  0.0 0.7 %slice.3 = bf16[16,256]{1,0:T(8,128)(2,1)S(1)} slice(bf16[512,256]{1,0:T(8,128)(2,1)} %tokens_ref.1), slice={[496:512], [0:256]} | slice | bytes 16384 | tf_op jit(solution)/shard_map/slice | solution.py:333
  0.7 1.6 %collective-permute-start = (bf16[16,256]{1,0:T(8,128)(2,1)S(1)}, bf16[16,256]{1,0:T(8,128)(2,1)S(1)}, u32[]{:S(2)}, u32[]{:S(2)}) collective-permute-start(bf16[16,256]{1,0:T(8,128)(2,1)S(1)} %slice.3), channel_id=1, source_target_pairs={{0,1},{1,2},{2,3},{3,4},{4,5},{5,6},{6,7},{7,8},{8,9},{9,10},{10,1... | collective-permute-start | bytes 24584 | tf_op jit(solution)/shard_map/ppermute | solution.py:322
  2.3 0.1 add_convert_fusion
  2.4 0.1 broadcast_in_dim.2.there_ref
  2.4 1.8 %project.1 = (bf16[256,512]{1,0:T(8,128)(2,1)S(1)}, f32[8,512]{1,0:T(8,128)S(1)}, bf16[256,512]{1,0:T(8,128)(2,1)S(1)}, f32[3,768]{1,0:T(4,128)S(1)}) custom-call(bf16[512,256]{1,0:T(8,128)(2,1)} %tokens_ref.1, bf16[256,768]{1,0:T(8,128)(2,1)} %w_ref.1, f32[3,768]{1,0:T(4,128)} %taps_ref.1), custom_call_target="tpu_custom_call" | custom-call | flops 134217728 | bytes 2097152 | tf_op jit(solution)/shard_map/project/pallas_call | solution.py:82
  4.2 5.9 %collective-permute-done.rim_ref = bf16[16,256]{1,0:T(8,128)(2,1)S(1)} collective-permute-done((bf16[16,256]{1,0:T(8,128)(2,1)S(1)}, bf16[16,256]{1,0:T(8,128)(2,1)S(1)}, u32[]{:S(2)}, u32[]{:S(2)}) %collective-permute-start) | collective-permute-done | bytes 8224 | tf_op jit(solution)/shard_map/ppermute | solution.py:322
  10.0 0.3 fix_rim.1
  10.3 0.0 copy-start
  10.3 0.0 copy-start.6
  10.3 15.9 %all_to_all.10.own_ref = bf16[16,16,512]{2,1,0:T(8,128)(2,1)S(1)} all-to-all(bf16[16,16,512]{2,1,0:T(8,128)(2,1)S(1)} %bitcast.5), channel_id=1, replica_groups=mesh['span'=16,'tok'=16] {'tok'}, dimensions={0} | all-to-all | bytes 524288 | tf_op jit(solution)/shard_map/all_to_all | solution.py:337
  26.3 0.0 collective-permute-start.1
  26.3 0.7 %copy-done.12 = f32[16]{0:T(128)S(1)} copy-done((f32[16]{0:T(128)S(1)}, f32[16]{0:T(128)}, u32[]{:S(2)}) %copy-start.12) | copy-done | bytes 88
  26.9 0.1 copy.14.gain_ref
  27.0 0.0 copy-start.5
  27.0 0.0 copy-start.7
  27.0 0.0 copy-start.9
  27.0 0.0 copy-start.10
  27.1 0.0 copy-start.11
  27.1 0.4 make_query.1.query_ref
  27.4 0.4 copy-done.5
  27.8 0.0 copy-done.7
  27.9 0.2 copy-done.9
  28.0 0.1 copy-done.10
  28.1 0.0 copy-done.11
  28.2 1.4 %early.1 = (f32[1024,256]{1,0:T(8,128)S(1)}, f32[1024,256]{1,0:T(8,128)S(1)}, f32[16,16,512]{2,1,0:T(8,128)S(1)}) custom-call(bf16[16,8192]{1,0:T(8,128)(2,1)S(1)} %copy-done.9, bf16[16,16,512]{2,1,0:T(8,128)(2,1)S(1)} %all_to_all.10.own_ref, f32[16,1]{1,0:T(8,128)S(1)} %copy.14.gain_ref, bf16[128,128]{1,0:T(8,128)(2,1)S(1)} %copy-done.7, ...), custom_call_target="tpu_custom_call" | custom-call | flops 800000000 | bytes 3145728 | tf_op jit(solution)/shard_map/early/pallas_call | solution.py:219
  29.5 4.9 %collective-permute-done.1.past_ref = bf16[16,16,512]{2,1,0:T(8,128)(2,1)S(1)} collective-permute-done((bf16[16,16,512]{2,1,0:T(8,128)(2,1)S(1)}, bf16[16,16,512]{2,1,0:T(8,128)(2,1)S(1)}, u32[]{:S(2)}, u32[]{:S(2)}) %collective-permute-start.1) | collective-permute-done | bytes 262176 | tf_op jit(solution)/shard_map/ppermute | solution.py:322
  34.5 0.0 copy-done.4
  34.5 1.0 %convolve.1 = bf16[16,16,512]{2,1,0:T(8,128)(2,1)S(1)} custom-call(f32[2,256]{1,0:T(2,128)S(1)} %broadcast_in_dim.2.there_ref, bf16[16,16,512]{2,1,0:T(8,128)(2,1)S(1)} %collective-permute-done.1.past_ref, f32[1024,256]{1,0:T(8,128)S(1)} %get-tuple-element.28.spec_ref, f32[1024,256]{1,0:T(8,128)S(1)} %get-tuple-element.30.freq_ref, ...), custom_call_target="tpu_custom_call" | custom-call | flops 800000000 | bytes 4194304 | tf_op jit(solution)/shard_map/convolve/pallas_call | solution.py:274
  35.5 0.0 copy-start.2
  35.5 13.7 %all_to_all.11 = bf16[16,16,512]{2,1,0:T(8,128)(2,1)S(1)} all-to-all(bf16[16,16,512]{2,1,0:T(8,128)(2,1)S(1)} %convolve.1), channel_id=1, replica_groups=mesh['span'=16,'tok'=16] {'tok'}, dimensions={0} | all-to-all | bytes 524288 | tf_op jit(solution)/shard_map/all_to_all | solution.py:345
  49.2 0.0 copy-done.2
  49.2 1.0 %project_out.1 = bf16[512,256]{1,0:T(8,128)(2,1)} custom-call(bf16[256,512]{1,0:T(8,128)(2,1)S(1)} %bitcast.6, f32[512,256]{1,0:T(8,128)S(1)} %make_query.1.query_ref, bf16[256,256]{1,0:T(8,128)(2,1)S(1)} %copy-done.2), custom_call_target="tpu_custom_call" | custom-call | flops 67108864 | bytes 2097152 | tf_op jit(solution)/shard_map/project_out/pallas_call | solution.py:304
  (10 shorter events, 0.0 us)
Async XLA Ops:
  0.7 9.3 %collective-permute-start = (bf16[16,256]{1,0:T(8,128)(2,1)S(1)}, bf16[16,256]{1,0:T(8,128)(2,1)S(1)}, u32[]{:S(2)}, u32[]{:S(2)}) collective-permute-start(bf16[16,256]{1,0:T(8,128)(2,1)S(1)} %slice.3), channel_id=1, source_target_pairs={{0,1},{1,2},{2,3},{3,4},{4,5},{5,6},{6,7},{7,8},{8,9},{9,10},{10,1... | collective-permute-start | bytes 24584 | tf_op jit(solution)/shard_map/ppermute | solution.py:322
  10.0 17.0 %copy-start.1 = (bf16[512,256]{1,0:T(8,128)(2,1)S(1)}, bf16[512,256]{1,0:T(8,128)(2,1)}, u32[]{:S(2)}) copy-start(bf16[512,256]{1,0:T(8,128)(2,1)} %tokens_ref.1) | copy-start | bytes 786436
  10.3 16.7 %copy-start = (bf16[256,768]{1,0:T(8,128)(2,1)S(1)}, bf16[256,768]{1,0:T(8,128)(2,1)}, u32[]{:S(2)}) copy-start(bf16[256,768]{1,0:T(8,128)(2,1)} %w_ref.1) | copy-start | bytes 1179652
  10.3 16.7 %copy-start.6 = (f32[3,768]{1,0:T(4,128)S(1)}, f32[3,768]{1,0:T(4,128)}, u32[]{:S(2)}) copy-start(f32[3,768]{1,0:T(4,128)} %taps_ref.1) | copy-start | bytes 27652
  26.3 0.7 %copy-start.12 = (f32[16]{0:T(128)S(1)}, f32[16]{0:T(128)}, u32[]{:S(2)}) copy-start(f32[16]{0:T(128)} %param.17) | copy-start | bytes 196
  26.3 8.2 %collective-permute-start.1 = (bf16[16,16,512]{2,1,0:T(8,128)(2,1)S(1)}, bf16[16,16,512]{2,1,0:T(8,128)(2,1)S(1)}, u32[]{:S(2)}, u32[]{:S(2)}) collective-permute-start(bf16[16,16,512]{2,1,0:T(8,128)(2,1)S(1)} %all_to_all.10.own_ref), channel_id=1, source_target_pairs={{0,16},{16,32},{32,48},{48,64},{64,80},{80,96},{96,112},{112,128},... | collective-permute-start | bytes 786440 | tf_op jit(solution)/shard_map/ppermute | solution.py:322
  27.0 0.8 %copy-start.5 = (f32[2,64,128]{2,1,0:T(8,128)S(1)}, f32[2,64,128]{2,1,0:T(8,128)}, u32[]{:S(2)}) copy-start(f32[2,64,128]{2,1,0:T(8,128)} %constant.29.clone.twist_ref) | copy-start | bytes 196612
  27.0 0.8 %copy-start.7 = (bf16[128,128]{1,0:T(8,128)(2,1)S(1)}, bf16[128,128]{1,0:T(8,128)(2,1)}, u32[]{:S(2)}) copy-start(bf16[128,128]{1,0:T(8,128)(2,1)} %constant.23.clone.into_lo_ref) | copy-start | bytes 98308
  27.0 1.0 %copy-start.9 = (bf16[16,8192]{1,0:T(8,128)(2,1)S(1)}, bf16[16,8192]{1,0:T(8,128)(2,1)}, u32[]{:S(2)}) copy-start(bf16[16,8192]{1,0:T(8,128)(2,1)} %filter_ref.1) | copy-start | bytes 786436
  27.0 1.1 %copy-start.10 = (bf16[768,256]{1,0:T(8,128)(2,1)S(1)}, bf16[768,256]{1,0:T(8,128)(2,1)}, u32[]{:S(2)}) copy-start(bf16[768,256]{1,0:T(8,128)(2,1)} %constant.26.clone.cols_in_ref) | copy-start | bytes 1179652
  27.1 1.1 %copy-start.11 = (bf16[128,128]{1,0:T(8,128)(2,1)S(1)}, bf16[128,128]{1,0:T(8,128)(2,1)}, u32[]{:S(2)}) copy-start(bf16[128,128]{1,0:T(8,128)(2,1)} %constant.24.clone.into_hi_ref) | copy-start | bytes 98308
  28.1 6.3 %copy-start.3 = (bf16[256,256]{1,0:T(8,128)(2,1)S(1)}, bf16[256,256]{1,0:T(8,128)(2,1)}, u32[]{:S(2)}) copy-start(bf16[256,256]{1,0:T(8,128)(2,1)} %constant.25.clone.cols_in_ref) | copy-start | bytes 393220
  28.1 6.3 %copy-start.4 = (bf16[256,256]{1,0:T(8,128)(2,1)S(1)}, bf16[256,256]{1,0:T(8,128)(2,1)}, u32[]{:S(2)}) copy-start(bf16[256,256]{1,0:T(8,128)(2,1)} %constant.27.clone.cols_out_ref) | copy-start | bytes 393220
  28.1 6.3 %copy-start.8 = (bf16[64,256]{1,0:T(8,128)(2,1)S(1)}, bf16[64,256]{1,0:T(8,128)(2,1)}, u32[]{:S(2)}) copy-start(bf16[64,256]{1,0:T(8,128)(2,1)} %constant.28.clone.back_ref) | copy-start | bytes 98308
  35.5 13.8 %copy-start.2 = (bf16[256,256]{1,0:T(8,128)(2,1)S(1)}, bf16[256,256]{1,0:T(8,128)(2,1)}, u32[]{:S(2)}) copy-start(bf16[256,256]{1,0:T(8,128)(2,1)} %w_ref.2) | copy-start | bytes 393220
